TPU v7x, 256 devices: a whole 4x4x8 slice. The times are simulated.
256 devices in a mesh: dp: 32 (over z, y), seq: 8 (over x, core).
Axes of the slice: x: 4, y: 4, z: 8, core: 2. Of those that a mesh axis runs over, the one named last changes fastest.
Arguments:
- slot_tokens: bfloat16 [416, 512, 1152], P('dp', 'seq'), may hold values from -12 to 12
- modulation: float32 [32, 6, 1152], P('dp'), may hold values from -2.5 to 2.5
- counts: int32 [32], replicated, may hold values from 1 to 13, as said below
- dest: int32 [32, 13], replicated, may hold values from 0 to 223, as said below
- qkv_spatial: bfloat16 [1152, 1728], replicated, may hold values from -4 to 4
- out_spatial: bfloat16 [576, 1152], replicated, may hold values from -0.25 to 0.25
- qkv_temporal: bfloat16 [1152, 1728], replicated, may hold values from -4 to 4
- out_temporal: bfloat16 [576, 1152], replicated, may hold values from -0.25 to 0.25
Outputs:
- video_out: bfloat16 [224, 512, 1152], P('dp', 'seq')
Inputs may be any that keep to these rules, and one draw needn't show every extreme that they name: Group g holds blocks in slots 0 to counts[g] - 1; the counts sum to 224; some group holds 13 blocks. Over the slots q below counts[g] of all groups g, dest[g, q] takes every value 0 to 223 exactly once; one group sends at most 1 block to one video, and some group sends 1; entries at slots from counts[g] on are arbitrary values of the same range.
All inputs are finite; a program needn't handle non-finite values.
Results may differ from a plain program's by a relative error of at most 0.0057.
Values may be sent and summed in bfloat16 or wider, within the bound.
No kernel may reach another device: no remote copies, remote signals or barrier semaphores. Data moves between devices by JAX's collectives and lax.ppermute only.
A program may use at most 64 MiB of HBM per device.

v0:
```python
import math

import jax
import jax.numpy as jnp
from jax import lax
from jax.sharding import PartitionSpec as P

HEADS = 8
HEAD_DIM = 72
NFD = 7


epsilon = 1e-06


def norm_mod(tokens, shift_row, scale_row):
    values = tokens.astype(jnp.float32)
    center = values - jnp.mean(values, axis=-1, keepdims=True)
    spread = jnp.mean(center * center, axis=-1, keepdims=True)
    return (center * lax.rsqrt(spread + epsilon) * (1.0 + scale_row) + shift_row).astype(
        jnp.bfloat16
    )


def attention(qkv_rows, batch_count, length):
    parts = qkv_rows.reshape(batch_count, length, 3, HEADS, HEAD_DIM)
    factor = 1.0 / math.sqrt(HEAD_DIM)
    scores = (
        jnp.einsum(
            "bqhs,bkhs->bhqk", parts[:, :, 0], parts[:, :, 1], preferred_element_type=jnp.float32
        )
        * factor
    )
    highest = jnp.max(scores, axis=-1, keepdims=True)
    raised = jnp.exp(scores - highest)
    weights = (raised / jnp.sum(raised, axis=-1, keepdims=True)).astype(jnp.bfloat16)
    mixed = jnp.einsum(
        "bhqk,bkhs->bqhs", weights, parts[:, :, 2], preferred_element_type=jnp.float32
    )
    return mixed.astype(jnp.bfloat16).reshape(batch_count * length, HEADS * HEAD_DIM)


def spatial_block(frames, modulation_rows, w_qkv, w_out):
    frame_count, patch_count, model_width = frames.shape
    shift_rows = modulation_rows[:, 0][:, None, :]
    scale_rows = modulation_rows[:, 1][:, None, :]
    gate_rows = modulation_rows[:, 2][:, None, :]
    normed = norm_mod(frames, shift_rows, scale_rows)
    qkv_rows = jnp.dot(
        normed.reshape(-1, model_width), w_qkv, preferred_element_type=jnp.float32
    ).astype(jnp.bfloat16)
    mixed = attention(qkv_rows, frame_count, patch_count)
    projected = jnp.dot(mixed, w_out, preferred_element_type=jnp.float32).reshape(
        frame_count, patch_count, model_width
    )
    return (frames.astype(jnp.float32) + gate_rows * projected).astype(jnp.bfloat16)


def on_device(
    slot_tokens, modulation, counts, dest, qkv_spatial, out_spatial, qkv_temporal, out_temporal
):
    group_count = lax.axis_size("dp")
    slot_count, patch_count, model_width = slot_tokens.shape
    block_count = NFD
    send_room = (slot_count + group_count - 1) // group_count
    group_index = lax.axis_index("dp")
    slot_ids = jnp.arange(slot_count, dtype=jnp.int32)
    group_ids = jnp.arange(group_count, dtype=jnp.int32)
    room_ids = jnp.arange(send_room, dtype=jnp.int32)
    live_slots = slot_ids[None, :] < counts[:, None]
    target_group = dest // block_count
    earlier = slot_ids[:, None] < slot_ids[None, :]
    same_target = (
        live_slots[:, :, None]
        & (target_group[:, :, None] == target_group[:, None, :])
        & earlier[None, :, :]
    )
    send_rank = jnp.sum(same_target.astype(jnp.int32), axis=1)
    own_live = lax.dynamic_index_in_dim(
        live_slots.astype(jnp.int32), group_index, 0, keepdims=False
    )
    own_target = lax.dynamic_index_in_dim(target_group, group_index, 0, keepdims=False)
    own_rank = lax.dynamic_index_in_dim(send_rank, group_index, 0, keepdims=False)
    picks = (
        (own_live[:, None, None] > 0)
        & (own_target[:, None, None] == group_ids[None, :, None])
        & (own_rank[:, None, None] == room_ids[None, None, :])
    )
    chosen_slot = jnp.sum(picks.astype(jnp.int32) * slot_ids[:, None, None], axis=0).reshape(-1)
    video_rows = lax.all_gather(modulation, "dp", axis=0, tiled=True)
    slot_modulation = jnp.take(video_rows, own_target, axis=0)
    processed = spatial_block(slot_tokens, slot_modulation, qkv_spatial, out_spatial)
    payload = jnp.take(processed, chosen_slot, axis=0)
    arrived = lax.all_to_all(payload, "dp", split_axis=0, concat_axis=0, tiled=True)
    wanted = group_index * block_count + jnp.arange(block_count, dtype=jnp.int32)
    matches = (live_slots[:, :, None] & (dest[:, :, None] == wanted[None, None, :])).astype(
        jnp.int32
    )
    source_group = jnp.sum(matches * group_ids[:, None, None], axis=(0, 1))
    source_rank = jnp.sum(matches * send_rank[:, :, None], axis=(0, 1))
    placed = jnp.take(arrived, source_group * send_room + source_rank, axis=0)
    own_modulation = modulation[0]
    shard_count = lax.axis_size("seq")
    widest = patch_count // shard_count
    frame_total = shard_count * block_count
    channels = placed.shape[-1]
    selected = placed.reshape(block_count, shard_count, widest, channels)
    moved = lax.all_to_all(selected, "seq", split_axis=1, concat_axis=0, tiled=True)
    token_rows = moved.reshape(frame_total * widest, channels)
    normed_rows = norm_mod(token_rows, own_modulation[3], own_modulation[4])
    qkv_rows = jnp.dot(normed_rows, qkv_temporal, preferred_element_type=jnp.float32).astype(
        jnp.bfloat16
    )
    qkv_width = qkv_rows.shape[-1]
    by_patch = (
        qkv_rows.reshape(frame_total, widest, qkv_width)
        .transpose(1, 0, 2)
        .reshape(widest * frame_total, qkv_width)
    )
    mixed = attention(by_patch, widest, frame_total)
    attn_width = mixed.shape[-1]
    mixed = (
        mixed.reshape(widest, frame_total, attn_width)
        .transpose(1, 0, 2)
        .reshape(frame_total * widest, attn_width)
    )
    projected_rows = jnp.dot(mixed, out_temporal, preferred_element_type=jnp.float32)
    homeward = (token_rows.astype(jnp.float32) + own_modulation[5] * projected_rows).astype(
        jnp.bfloat16
    )
    back_width = homeward.shape[-1]
    returned = lax.all_to_all(
        homeward.reshape(frame_total, 1, widest, back_width),
        "seq",
        split_axis=0,
        concat_axis=1,
        tiled=True,
    )
    restored = returned.reshape(block_count, patch_count, back_width)
    return restored


def solution(mesh):
    in_specs = (P("dp", "seq", None), P("dp", None, None), P(), P(), P(), P(), P(), P())
    out_specs = P("dp", "seq", None)
    return jax.shard_map(
        on_device, mesh=mesh, in_specs=in_specs, out_specs=out_specs, check_vma=False
    )
```

profile of v0, /device:TPU:1, one launch (start us, length us, event | category | flops | bytes accessed | tf_op | source)
XLA Modules:
  0.0 281.3 jit_solution(13004928788901511606)
XLA Ops:
  0.0 0.9 add_select_fusion
  0.9 0.2 dynamic-slice_reduce_fusion
  1.1 0.7 iota_compare_fusion.1
  1.9 0.2 fusion.37
  2.0 0.1 fusion.39
  2.2 0.8 copy.83
  3.0 47.9 %all_gather.3 = f32[32,6,1152]{2,1,0:T(8,128)} all-gather(f32[1,6,1152]{2,1,0:T(8,128)S(1)} %copy.83), channel_id=1, replica_groups=mesh['dp'=32,'seq'=8] {'dp'}, dimensions={0}, use_global_device_ids=true | all-gather | bytes 912384 | tf_op jit(solution)/shard_map/all_gather | solution.py:90
  50.9 2.6 gather_fusion
  53.5 1.1 broadcast_select_fusion.1
  54.6 0.1 fusion.47
  54.8 0.3 convert_reduce_fusion
  55.1 0.6 fusion.4
  55.8 1.0 fusion.7
  56.8 1.1 copy-done.6
  57.9 5.4 %convolution_convert_fusion = bf16[832,1728]{1,0:T(8,128)(2,1)} fusion(bf16[832,1152]{1,0:T(8,128)(2,1)S(1)} %bitcast.123, bf16[1152,1728]{0,1:T(8,128)(2,1)S(1)} %copy-done.6), kind=kOutput, calls=%fused_computation.17 | convolution fusion | flops 3313889280 | bytes 8773632 | tf_op jit(solution)/shard_map/dot_general | solution.py:49
  63.4 9.2 %reshape.348 = bf16[13,64,3,8,72]{4,3,2,1,0:T(8,128)(2,1)} reshape(bf16[832,1728]{1,0:T(8,128)(2,1)} %convolution_convert_fusion) | data formatting | bytes 5750784 | tf_op jit(solution)/shard_map/reshape | solution.py:26
  72.6 2.8 fusion.45
  75.4 1.0 fusion.23
  76.4 5.0 %fusion.48 = (f32[13,8,64]{2,1,0:T(8,128)S(1)}, f32[13,8,64,64]{2,3,1,0:T(8,128)S(1)}) fusion(f32[13,8,64,64]{2,3,1,0:T(8,128)S(1)} %fusion.23), kind=kOutput, calls=%fused_computation.116 | output fusion | flops 1703999 | bytes 3434496 | tf_op jit(solution)/shard_map/sub | solution.py:35
  81.5 0.9 fusion.26
  82.3 2.6 copy.88
  84.9 3.8 %dot_general.29 = bf16[13,64,576]{2,1,0:T(8,128)(2,1)} reshape(bf16[13,64,8,72]{3,2,1,0:T(8,128)(2,1)} %copy.88) | data formatting | bytes 1916928 | tf_op jit(solution)/shard_map/dot_general | solution.py:53
  88.8 4.3 %fusion.8 = bf16[13,64,1152]{2,1,0:T(8,128)(2,1)} fusion(bf16[13,64,576]{2,1,0:T(8,128)(2,1)} %dot_general.29, bf16[13,64,1152]{2,1,0:T(8,128)(2,1)S(1)} %copy-done.2, f32[13,1152]{1,0:T(8,128)S(1)} %bitcast.124, bf16[576,1152]{1,0:T(8,128)(2,1)S(1)} %copy-done), kind=kOutput, calls=%fused_computation.16 | convolution fusion | flops 1107984384 | bytes 6179328 | tf_op jit(solution)/shard_map/dot_general | solution.py:53
  93.1 4.8 %gather_fusion.1 = bf16[32,64,1152]{2,1,0:T(8,128)(2,1)} fusion(bf16[13,64,1152]{2,1,0:T(8,128)(2,1)} %fusion.8, s32[1024]{0:T(1024)S(1)} %pad_clamp_fusion.1), kind=kCustom, calls=%fused_computation.1 | custom fusion | bytes 9437312 | tf_op jit(solution)/shard_map/jit(_take)/gather | solution.py:93
  97.8 5.0 %broadcast_select_fusion = bf16[32,64,1152]{2,1,0:T(8,128)(2,1)} fusion(bf16[32,64,1152]{2,1,0:T(8,128)(2,1)} %gather_fusion.1, pred[32]{0:T(512)(128)(4,1)S(1)} %compare_and_fusion.2), kind=kLoop, calls=%fused_computation.8 | loop fusion | flops 2359296 | bytes 9437216 | tf_op jit(solution)/shard_map/jit(_take)/select_n | solution.py:93
  102.9 5.7 %all-to-all-start = ((bf16[32,64,1152]{2,1,0:T(8,128)(2,1)}), bf16[32,64,1152]{2,1,0:T(8,128)(2,1)}, u32[]{:S(2)}, u32[]{:S(2)}) async-start(bf16[32,64,1152]{2,1,0:T(8,128)(2,1)} %broadcast_select_fusion), calls=%async_computation | async-start | bytes 9437184 | tf_op jit(solution)/shard_map/all_to_all | solution.py:94
  108.6 0.2 select_reduce_fusion
  108.8 93.4 %all-to-all-done = bf16[32,64,1152]{2,1,0:T(8,128)(2,1)} async-done(((bf16[32,64,1152]{2,1,0:T(8,128)(2,1)}), bf16[32,64,1152]{2,1,0:T(8,128)(2,1)}, u32[]{:S(2)}, u32[]{:S(2)}) %all-to-all-start) | async-done | bytes 4718624 | tf_op jit(solution)/shard_map/all_to_all | solution.py:94
  202.2 3.0 %gather_fusion.2 = bf16[7,64,1152]{2,1,0:T(8,128)(2,1)S(1)} fusion(bf16[32,64,1152]{2,1,0:T(8,128)(2,1)} %all-to-all-done, s32[1024]{0:T(1024)S(1)} %pad_clamp_fusion), kind=kCustom, calls=%fused_computation.2 | custom fusion | bytes 2064412 | tf_op jit(solution)/shard_map/jit(_take)/gather | solution.py:101
  205.3 1.3 copy_select_fusion
  206.6 18.9 %all-to-all-start.1 = ((bf16[7,8,8,1152]{3,2,0,1:T(8,128)(2,1)}), bf16[7,8,8,1152]{3,2,0,1:T(8,128)(2,1)S(1)}, u32[]{:S(2)}, u32[]{:S(2)}) async-start(bf16[7,8,8,1152]{3,2,0,1:T(8,128)(2,1)} %copy_select_fusion), calls=%async_computation.1 | async-start | bytes 2064384 | tf_op jit(solution)/shard_map/all_to_all | solution.py:108
  225.5 14.7 %all-to-all-done.1 = bf16[7,8,8,1152]{3,2,0,1:T(8,128)(2,1)S(1)} async-done(((bf16[7,8,8,1152]{3,2,0,1:T(8,128)(2,1)}), bf16[7,8,8,1152]{3,2,0,1:T(8,128)(2,1)S(1)}, u32[]{:S(2)}, u32[]{:S(2)}) %all-to-all-start.1) | async-done | bytes 1032224 | tf_op jit(solution)/shard_map/all_to_all | solution.py:108
  240.2 0.2 bitcast_reduce_fusion
  240.6 0.4 fusion.21
  241.1 0.5 fusion.19
  241.6 4.4 %fusion.15 = bf16[56,8,1728]{2,1,0:T(8,128)(2,1)S(1)} fusion(bf16[448,1152]{1,0:T(8,128)(2,1)S(1)} %fusion.19, bf16[1152,1728]{0,1:T(8,128)(2,1)} %param.14), kind=kOutput, calls=%fused_computation.27 | convolution fusion | flops 1784401920 | bytes 6561792 | tf_op jit(solution)/shard_map/dot_general | solution.py:111
  246.0 0.3 copy.163
  246.3 4.0 %reshape_reshape.6 = bf16[8,56,3,8,72]{4,3,2,1,0:T(8,128)(2,1)} reshape(bf16[8,56,1728]{2,1,0:T(8,128)(2,1)S(1)} %bitcast.120) | data formatting | bytes 3096576 | tf_op jit(solution)/shard_map/reshape;reshape | solution.py:26
  250.2 2.9 %fusion.46 = (bf16[8,56,1,8,72]{4,3,2,1,0:T(8,128)(2,1)S(1)}, bf16[8,56,1,8,72]{4,3,2,1,0:T(8,128)(2,1)S(1)}, bf16[8,56,1,8,72]{4,3,2,1,0:T(8,128)(2,1)}) fusion(bf16[8,56,3,8,72]{4,3,2,1,0:T(8,128)(2,1)} %reshape_reshape.6), kind=kLoop, calls=%fused_computation.114 | loop fusion | bytes 3096576 | tf_op jit(solution)/shard_map/slice | solution.py:38
  253.1 3.5 %fusion.49 = (f32[8,8,56]{2,1,0:T(8,128)S(1)}, f32[8,8,56,56]{2,3,1,0:T(8,128)}) fusion(bf16[8,56,1,8,72]{4,3,2,1,0:T(8,128)(2,1)} %get-tuple-element.15, bf16[8,56,1,8,72]{4,3,2,1,0:T(8,128)(2,1)S(1)} %get-tuple-element.14), kind=kOutput, calls=%fused_computation.117 | convolution fusion | flops 29503544 | bytes 1849344 | tf_op jit(solution)/shard_map/sub | solution.py:35
  256.6 2.2 fusion.27
  258.8 0.1 copy.100
  258.9 0.7 reshape_reshape.7
  259.6 0.1 bitcast_convert_fusion
  259.8 1.2 copy-done.3
  260.9 1.1 fusion.14
  262.0 18.2 %all_to_all.29 = bf16[56,1,8,1152]{3,2,1,0:T(8,128)(2,1)S(1)} all-to-all(bf16[56,1,8,1152]{3,2,1,0:T(8,128)(2,1)S(1)} %fusion.14), channel_id=1, replica_groups=mesh['dp'=32,'seq'=8] {'seq'}, dimensions={0} | all-to-all | bytes 2064384 | tf_op jit(solution)/shard_map/all_to_all | solution.py:132
  280.2 1.1 copy.164
  (35 shorter events, 0.5 us)
Async XLA Ops:
  0.0 88.8 %copy-start = (bf16[576,1152]{1,0:T(8,128)(2,1)S(1)}, bf16[576,1152]{1,0:T(8,128)(2,1)}, u32[]{:S(2)}) copy-start(bf16[576,1152]{1,0:T(8,128)(2,1)} %param.13) | copy-start | bytes 3981316
  0.0 54.8 %copy-start.2 = (bf16[13,64,1152]{2,1,0:T(8,128)(2,1)S(1)}, bf16[13,64,1152]{2,1,0:T(8,128)(2,1)}, u32[]{:S(2)}) copy-start(bf16[13,64,1152]{2,1,0:T(8,128)(2,1)} %param.8) | copy-start | bytes 5750788
  55.8 2.1 copy-start.6
  102.9 5.7 %copy-start.5 = (s32[32,13]{0,1:T(8,128)S(1)}, s32[32,13]{0,1:T(8,128)}, u32[]{:S(2)}) copy-start(s32[32,13]{0,1:T(8,128)} %param.11) | copy-start | bytes 4996
  102.9 99.4 %all-to-all-start = ((bf16[32,64,1152]{2,1,0:T(8,128)(2,1)}), bf16[32,64,1152]{2,1,0:T(8,128)(2,1)}, u32[]{:S(2)}, u32[]{:S(2)}) async-start(bf16[32,64,1152]{2,1,0:T(8,128)(2,1)} %broadcast_select_fusion), calls=%async_computation | async-start | bytes 9437184 | tf_op jit(solution)/shard_map/all_to_all | solution.py:94
  205.3 20.2 %copy-start.4 = (f32[1,6,1152]{2,0,1:T(1,128)S(1)}, f32[1,6,1152]{2,0,1:T(1,128)}, u32[]{:S(2)}) copy-start(f32[1,6,1152]{2,0,1:T(1,128)} %param.9) | copy-start | bytes 82948
  206.6 33.6 %all-to-all-start.1 = ((bf16[7,8,8,1152]{3,2,0,1:T(8,128)(2,1)}), bf16[7,8,8,1152]{3,2,0,1:T(8,128)(2,1)S(1)}, u32[]{:S(2)}, u32[]{:S(2)}) async-start(bf16[7,8,8,1152]{3,2,0,1:T(8,128)(2,1)} %copy_select_fusion), calls=%async_computation.1 | async-start | bytes 2064384 | tf_op jit(solution)/shard_map/all_to_all | solution.py:108
  259.6 1.3 copy-start.3
  260.9 20.3 %copy-start.1 = (bf16[576,1152]{1,0:T(8,128)(2,1)S(1)}, bf16[576,1152]{1,0:T(8,128)(2,1)}, u32[]{:S(2)}) copy-start(bf16[576,1152]{1,0:T(8,128)(2,1)} %param.13) | copy-start | bytes 3981316
where the time goes:
time: 282 us; the launch traced here: 281 us
  waiting for transfers between devices  108 us (38%)
  blocking collectives  66.1 us (23%)
  local copies, waits for them, and re-layouts  41.4 us (15%)
  starting transfers between devices  24.6 us (9%)
  matrix products  22.7 us (8%)
  other arithmetic  18.1 us (6%)
    all_to_all x1, waiting for transfers between devices, on_device(): lax.all_to_all(payload, 'dp', split_axis=0, concat_axis=0, tiled=True)  93.4 us
    all_gather x1, blocking collectives, on_device(): video_rows = lax.all_gather(modulation, 'dp', axis=0, tiled=True)  47.9 us
    all_to_all x1, starting transfers between devices, on_device(): lax.all_to_all(selected, 'seq', split_axis=1, concat_axis=0, tiled=True)  18.9 us
    all_to_all x1, blocking collectives, on_device(): lax.all_to_all(homeward.reshape(frame_total, 1, widest, back_width), 'seq...  18.2 us
    all_to_all x1, waiting for transfers between devices, on_device(): lax.all_to_all(selected, 'seq', split_axis=1, concat_axis=0, tiled=True)  14.7 us
    reshape x1, local copies, waits for them, and re-layouts, attention(): parts = qkv_rows.reshape(batch_count, length, 3, HEADS, HEAD_DIM)  9.25 us
    all_to_all x1, starting transfers between devices, on_device(): lax.all_to_all(payload, 'dp', split_axis=0, concat_axis=0, tiled=True)  5.7 us
    slice x2, local copies, waits for them, and re-layouts, attention(): parts[:, :, 2]  5.66 us
  transfers between devices with their start and end apart: 2, of which 2 were waited for; matrix products, arithmetic and copies ran while one was open for 0% of the time, Pallas kernels for 0%

commit v1 on v0

v1 whole, which is shorter than its diff:
```python
import math

import jax
import jax.numpy as jnp
from jax import lax
from jax.sharding import PartitionSpec as P

HEADS = 8
HEAD_DIM = 72
NFD = 7
EPS = 1e-06


def norm_mod(tokens, shift_row, scale_row):
    values = tokens.astype(jnp.float32)
    center = values - jnp.mean(values, axis=-1, keepdims=True)
    spread = jnp.mean(center * center, axis=-1, keepdims=True)
    return (center * lax.rsqrt(spread + EPS) * (1.0 + scale_row) + shift_row).astype(jnp.bfloat16)


def attention(qkv_rows, batch_count, length):
    parts = qkv_rows.reshape(batch_count, length, 3, HEADS, HEAD_DIM)
    factor = 1.0 / math.sqrt(HEAD_DIM)
    scores = (
        jnp.einsum("bqhs,bkhs->bhqk", parts[:, :, 0], parts[:, :, 1], preferred_element_type=jnp.float32)
        * factor
    )
    highest = jnp.max(scores, axis=-1, keepdims=True)
    raised = jnp.exp(scores - highest)
    weights = (raised / jnp.sum(raised, axis=-1, keepdims=True)).astype(jnp.bfloat16)
    mixed = jnp.einsum("bhqk,bkhs->bqhs", weights, parts[:, :, 2], preferred_element_type=jnp.float32)
    return mixed.astype(jnp.bfloat16).reshape(batch_count * length, HEADS * HEAD_DIM)


def block(rows, shift, scale, gate, w_qkv, w_out, attend):
    normed = norm_mod(rows, shift, scale)
    qkv = jnp.dot(normed, w_qkv, preferred_element_type=jnp.float32).astype(jnp.bfloat16)
    mixed = attend(qkv)
    projected = jnp.dot(mixed, w_out, preferred_element_type=jnp.float32)
    return (rows.astype(jnp.float32) + gate * projected).astype(jnp.bfloat16)


def source_index(counts, dest):
    groups, slots = dest.shape
    slot_ids = jnp.arange(slots, dtype=jnp.int32)
    live = slot_ids[None, :] < counts[:, None]
    targets = jnp.where(live, dest, -1).reshape(-1)
    wanted = jnp.arange(groups * NFD, dtype=jnp.int32)
    anchors = jnp.arange(groups * slots, dtype=jnp.int32)
    return jnp.sum(jnp.where(targets[None, :] == wanted[:, None], anchors[None, :], 0), axis=1)


def on_device(slot_tokens, modulation, counts, dest, qkv_spatial, out_spatial, qkv_temporal, out_temporal):
    groups = lax.axis_size("dp")
    shards = lax.axis_size("seq")
    slots, patches, width = slot_tokens.shape
    piece = patches // groups
    mod = modulation[0]
    pieces = slot_tokens.reshape(slots, groups, piece, width).transpose(1, 0, 2, 3)
    spread = lax.all_to_all(pieces, "dp", split_axis=0, concat_axis=0, tiled=True)
    chosen = jnp.take(spread.reshape(groups * slots, piece, width), source_index(counts, dest), axis=0)
    gathered = lax.all_to_all(
        chosen.reshape(groups, NFD, piece, width), "dp", split_axis=0, concat_axis=0, tiled=True
    )
    frames = gathered.transpose(1, 0, 2, 3).reshape(NFD * patches, width)
    after = block(
        frames, mod[0], mod[1], mod[2], qkv_spatial, out_spatial, lambda qkv: attention(qkv, NFD, patches)
    )
    widest = patches // shards
    total = shards * NFD
    moved = lax.all_to_all(
        after.reshape(NFD, shards, widest, width), "seq", split_axis=1, concat_axis=0, tiled=True
    )

    def attend(qkv):
        by_patch = qkv.reshape(total, widest, -1).transpose(1, 0, 2).reshape(widest * total, -1)
        mixed = attention(by_patch, widest, total)
        return mixed.reshape(widest, total, -1).transpose(1, 0, 2).reshape(total * widest, -1)

    home = block(
        moved.reshape(total * widest, width), mod[3], mod[4], mod[5], qkv_temporal, out_temporal, attend
    )
    back = lax.all_to_all(
        home.reshape(total, 1, widest, width), "seq", split_axis=0, concat_axis=1, tiled=True
    )
    return back.reshape(NFD, patches, width)


def solution(mesh):
    in_specs = (P("dp", "seq", None), P("dp", None, None), P(), P(), P(), P(), P(), P())
    return jax.shard_map(
        on_device, mesh=mesh, in_specs=in_specs, out_specs=P("dp", "seq", None), check_vma=False
    )
```

time: 282 us -> 210 us (0.74)
  waiting for transfers between devices: 108 us -> 68.9 us
  blocking collectives: 66.1 us -> 40.8 us
  other arithmetic: 18.1 us -> 7.6 us
  starting transfers between devices: 24.6 us -> 18.5 us
  matrix products: 22.7 us -> 28.4 us
    all_gather x1 -> x0, blocking collectives: 47.9 us -> none  [on_device(): video_rows = lax.all_gather(modulation, 'dp', axis=0, tiled=True)]
    all_to_all x2, waiting for transfers between devices: 108 us -> 68.9 us  [the longest x1 44.3 us: on_device(): lax.all_to_all(pieces, 'dp', split_axis=0, concat_axis=0, tiled=True)]
    all_to_all x1 -> x2, blocking collectives: 18.2 us -> 40.8 us  [the longest x1 22.6 us: on_device(): lax.all_to_all(after.reshape(NFD, shards, widest, width), 'seq', split_ax...]
    reshape x1 -> x5, local copies, waits for them, and re-layouts: 0.27 us -> 10.8 us  [the longest x2 6.72 us: on_device(): slot_tokens.reshape(slots, groups, piece, width).transpose(1, 0, 2, 3)]
    gather x3 -> x1, local copies, waits for them, and re-layouts: 10.4 us -> 3.75 us  [on_device(): jnp.take(spread.reshape(groups * slots, piece, width), source_index(count...]
    all_to_all x2, starting transfers between devices: 24.6 us -> 18.5 us  [the longest x1 12.2 us: on_device(): lax.all_to_all(pieces, 'dp', split_axis=0, concat_axis=0, tiled=True)]
    select_n x7 -> x3, other arithmetic: 8.34 us -> 2.99 us  [the longest x2 2.98 us: on_device(): jnp.take(spread.reshape(groups * slots, piece, width), source_index(count...]
    sub x1 -> x0, other arithmetic: 5.03 us -> none  [attention(): raised = jnp.exp(scores - highest)]
where the time goes in v1:
time: 210 us; the launch traced here: 209 us
  waiting for transfers between devices  68.9 us (33%)
  local copies, waits for them, and re-layouts  44.2 us (21%)
  blocking collectives  40.8 us (19%)
  matrix products  28.4 us (14%)
  starting transfers between devices  18.5 us (9%)
  other arithmetic  7.6 us (4%)
    all_to_all x1, waiting for transfers between devices, on_device(): lax.all_to_all(pieces, 'dp', split_axis=0, concat_axis=0, tiled=True)  44.3 us
    all_to_all x1, waiting for transfers between devices, on_device(): lax.all_to_all(chosen.reshape(groups, NFD, piece, width), 'dp', split_axi...  24.6 us
    all_to_all x1, blocking collectives, on_device(): lax.all_to_all(after.reshape(NFD, shards, widest, width), 'seq', split_ax...  22.6 us
    all_to_all x1, blocking collectives, on_device(): lax.all_to_all(home.reshape(total, 1, widest, width), 'seq', split_axis=0...  18.2 us
    all_to_all x1, starting transfers between devices, on_device(): lax.all_to_all(pieces, 'dp', split_axis=0, concat_axis=0, tiled=True)  12.2 us
    dot_general x2, matrix products, block(): jnp.dot(normed, w_qkv, preferred_element_type=jnp.float32)  10.1 us
    reshape x2, local copies, waits for them, and re-layouts, on_device(): slot_tokens.reshape(slots, groups, piece, width).transpose(1, 0, 2, 3)  6.72 us
    all_to_all x1, starting transfers between devices, on_device(): lax.all_to_all(chosen.reshape(groups, NFD, piece, width), 'dp', split_axi...  6.37 us
  transfers between devices with their start and end apart: 2, of which 2 were waited for; matrix products, arithmetic and copies ran while one was open for 0% of the time, Pallas kernels for 0%

profile of v1, /device:TPU:1, one launch (start us, length us, event | category | flops | bytes accessed | tf_op | source)
XLA Modules:
  0.0 208.7 jit_solution(6715903901294689120)
XLA Ops:
  0.0 4.1 %reshape.163 = bf16[13,32,2,1152]{3,2,1,0:T(2,128)(2,1)S(1)} reshape(bf16[13,64,1152]{2,1,0:T(8,128)(2,1)} %param.8) | data formatting | bytes 3833856 | tf_op jit(solution)/shard_map/reshape | solution.py:59
  4.1 2.6 %copy.180 = bf16[13,32,2,1152]{3,2,0,1:T(2,128)(2,1)} copy(bf16[13,32,2,1152]{3,2,1,0:T(2,128)(2,1)S(1)} %reshape.163) | data formatting | bytes 3833856 | tf_op jit(solution)/shard_map/reshape | solution.py:59
  6.7 12.2 %all-to-all-start = ((bf16[32,13,2,1152]{3,2,1,0:T(2,128)(2,1)}), bf16[32,13,2,1152]{3,2,1,0:T(2,128)(2,1)S(1)}, u32[]{:S(2)}, u32[]{:S(2)}) async-start(bf16[32,13,2,1152]{3,2,1,0:T(2,128)(2,1)} %bitcast.114), calls=%async_computation | async-start | bytes 3833856 | tf_op jit(solution)/shard_map/all_to_all | solution.py:60
  18.9 0.1 copy.85
  19.0 0.1 eq.15
  19.1 0.1 select_reduce_fusion
  19.3 0.1 reduce_sum.68
  19.4 44.3 %all-to-all-done = bf16[32,13,2,1152]{3,2,1,0:T(2,128)(2,1)S(1)} async-done(((bf16[32,13,2,1152]{3,2,1,0:T(2,128)(2,1)}), bf16[32,13,2,1152]{3,2,1,0:T(2,128)(2,1)S(1)}, u32[]{:S(2)}, u32[]{:S(2)}) %all-to-all-start) | async-done | bytes 1916960 | tf_op jit(solution)/shard_map/all_to_all | solution.py:60
  63.7 3.7 %gather_fusion = bf16[224,2,1152]{2,1,0:T(2,128)(2,1)} fusion(bf16[416,2,1152]{2,1,0:T(2,128)(2,1)S(1)} %bitcast.119, s32[1024]{0:T(1024)S(1)} %pad_clamp_fusion), kind=kCustom, calls=%fused_computation | custom fusion | bytes 2065280 | tf_op jit(solution)/shard_map/jit(_take)/gather | solution.py:61
  67.4 3.0 %broadcast_select_fusion = bf16[32,7,2,1152]{3,2,1,0:T(2,128)(2,1)} fusion(bf16[32,7,2,1152]{3,2,1,0:T(2,128)(2,1)} %bitcast.120, pred[32,7]{1,0:T(8,128)(4,1)S(1)} %compare_and_fusion), kind=kLoop, calls=%fused_computation.25 | loop fusion | flops 516096 | bytes 2064608 | tf_op jit(solution)/shard_map/jit(_take)/select_n | solution.py:61
  70.4 6.4 %all-to-all-start.1 = ((bf16[32,7,2,1152]{3,2,1,0:T(2,128)(2,1)}), bf16[32,7,2,1152]{3,2,1,0:T(2,128)(2,1)S(1)}, u32[]{:S(2)}, u32[]{:S(2)}) async-start(bf16[32,7,2,1152]{3,2,1,0:T(2,128)(2,1)} %broadcast_select_fusion), calls=%async_computation.1 | async-start | bytes 2064384 | tf_op jit(solution)/shard_map/all_to_all | solution.py:62
  76.9 24.6 %all-to-all-done.1 = bf16[32,7,2,1152]{3,2,1,0:T(2,128)(2,1)S(1)} async-done(((bf16[32,7,2,1152]{3,2,1,0:T(2,128)(2,1)}), bf16[32,7,2,1152]{3,2,1,0:T(2,128)(2,1)S(1)}, u32[]{:S(2)}, u32[]{:S(2)}) %all-to-all-start.1) | async-done | bytes 1032224 | tf_op jit(solution)/shard_map/all_to_all | solution.py:62
  101.5 0.9 fusion.18
  102.4 0.1 div.33
  102.6 1.5 multiply_reduce_fusion
  104.2 0.1 rsqrt.23
  104.3 0.7 convert_bitcast_fusion
  105.0 2.0 copy.87
  107.1 2.7 %reshape.172 = f32[448,1152]{1,0:T(8,128)S(1)} reshape(f32[7,32,2,1152]{3,2,1,0:T(2,128)} %copy.87) | data formatting | bytes 4128768 | tf_op jit(solution)/shard_map/convert_element_type | solution.py:40
  109.8 5.7 %convolution_convert_fusion.1 = bf16[448,1728]{1,0:T(8,128)(2,1)} fusion(bf16[1152,1728]{0,1:T(8,128)(2,1)} %param.12, f32[448,1152]{1,0:T(8,128)S(1)} %reshape.172, f32[1152]{0:T(1024)S(1)} %get-tuple-element.7, f32[1152]{0:T(1024)S(1)} %get-tuple-element.8, f32[448]{0:T(512)S(1)} %rsqrt.23, f32[448]{0:T(512)S(1)} %div.33), kind=kOutput, calls=%fused_computation.8 | convolution fusion | flops 1786982400 | bytes 7606784 | tf_op jit(solution)/shard_map/dot_general | solution.py:37
  115.4 5.4 %reshape.165 = bf16[7,64,3,8,72]{4,3,2,1,0:T(8,128)(2,1)} reshape(bf16[448,1728]{1,0:T(8,128)(2,1)} %convolution_convert_fusion.1) | data formatting | bytes 3096576 | tf_op jit(solution)/shard_map/reshape | solution.py:22
  120.9 3.3 %fusion.44 = (bf16[7,64,1,8,72]{4,3,2,1,0:T(8,128)(2,1)}, bf16[7,64,1,8,72]{4,3,2,1,0:T(8,128)(2,1)}, bf16[7,64,1,8,72]{4,3,2,1,0:T(8,128)(2,1)}) fusion(bf16[7,64,3,8,72]{4,3,2,1,0:T(8,128)(2,1)} %reshape.165), kind=kLoop, calls=%fused_computation.86 | loop fusion | bytes 3096576 | tf_op jit(solution)/shard_map/slice | solution.py:25
  124.2 2.3 %fusion.45 = f32[7,8,64]{2,1,0:T(8,128)S(1)} fusion(bf16[7,64,1,8,72]{4,3,2,1,0:T(8,128)(2,1)} %get-tuple-element.16, bf16[7,64,1,8,72]{4,3,2,1,0:T(8,128)(2,1)} %get-tuple-element.14), kind=kOutput, calls=%fused_computation.87 | convolution fusion | flops 33718336 | bytes 1046528 | tf_op jit(solution)/shard_map/sub | solution.py:29
  126.5 3.3 %fusion.24 = f32[7,8,64,64]{2,3,1,0:T(8,128)} fusion(bf16[7,64,1,8,72]{4,3,2,1,0:T(8,128)(2,1)} %get-tuple-element.16, bf16[7,64,1,8,72]{4,3,2,1,0:T(8,128)(2,1)} %get-tuple-element.14), kind=kOutput, calls=%fused_computation.52 | convolution fusion | flops 33030144 | bytes 1949696 | tf_op jit(solution)/shard_map/bqhs,bkhs->bhqk/dot_general | solution.py:25
  129.8 3.5 %fusion.16 = bf16[7,64,8,72]{3,1,2,0:T(8,128)(2,1)} fusion(bf16[7,64,1,8,72]{4,3,2,1,0:T(8,128)(2,1)} %get-tuple-element.15, f32[7,8,64]{2,1,0:T(8,128)S(1)} %fusion.45, f32[7,8,64,64]{2,3,1,0:T(8,128)} %fusion.24), kind=kOutput, calls=%fused_computation.38 | convolution fusion | flops 34209344 | bytes 1964032 | tf_op jit(solution)/shard_map/bhqk,bkhs->bqhs/dot_general | solution.py:31
  133.3 2.7 %copy.97 = bf16[7,64,8,72]{3,2,1,0:T(8,128)(2,1)} copy(bf16[7,64,8,72]{3,1,2,0:T(8,128)(2,1)} %fusion.16) | data formatting | bytes 1032192 | tf_op jit(solution)/shard_map/convert_element_type | solution.py:32
  136.1 2.6 %reshape.166 = bf16[448,576]{1,0:T(8,128)(2,1)} reshape(bf16[7,64,8,72]{3,2,1,0:T(8,128)(2,1)} %copy.97) | data formatting | bytes 1032192 | tf_op jit(solution)/shard_map/reshape | solution.py:32
  138.6 2.1 %fusion.4 = bf16[448,1152]{1,0:T(8,128)(2,1)S(1)} fusion(f32[448,1152]{1,0:T(8,128)S(1)} %reshape.172, bf16[448,576]{1,0:T(8,128)(2,1)} %reshape.166, bf16[576,1152]{1,0:T(8,128)(2,1)S(1)} %copy-done, f32[1152]{0:T(1024)S(1)} %get-tuple-element.9), kind=kOutput, calls=%fused_computation.9 | convolution fusion | flops 596090880 | bytes 4944384 | tf_op jit(solution)/shard_map/dot_general | solution.py:39
  140.8 22.6 %all_to_all.34 = bf16[7,8,8,1152]{3,2,0,1:T(8,128)(2,1)S(1)} all-to-all(bf16[7,8,8,1152]{3,2,0,1:T(8,128)(2,1)S(1)} %copy.98), channel_id=1, replica_groups=mesh['dp'=32,'seq'=8] {'seq'}, dimensions={1} | all-to-all | bytes 2064384 | tf_op jit(solution)/shard_map/all_to_all | solution.py:71
  163.4 0.2 bitcast_reduce_fusion
  163.7 0.1 div.38
  163.8 0.4 fusion.13
  164.2 0.1 rsqrt.25
  164.3 0.5 fusion.11
  164.8 4.4 %fusion.7 = bf16[56,8,1728]{2,1,0:T(8,128)(2,1)S(1)} fusion(bf16[448,1152]{1,0:T(8,128)(2,1)S(1)} %fusion.11, bf16[1152,1728]{0,1:T(8,128)(2,1)} %param.14), kind=kOutput, calls=%fused_computation.12 | convolution fusion | flops 1784401920 | bytes 6561792 | tf_op jit(solution)/shard_map/dot_general | solution.py:37
  169.2 1.4 copy.181
  170.6 5.4 %reshape_reshape.6 = bf16[8,56,3,8,72]{4,3,2,1,0:T(8,128)(2,1)} reshape(bf16[8,56,1728]{2,1,0:T(8,128)(2,1)} %bitcast.118) | data formatting | bytes 3096576 | tf_op jit(solution)/shard_map/reshape;reshape | solution.py:22
  176.0 3.2 %fusion.43 = (bf16[8,56,1,8,72]{4,3,2,1,0:T(8,128)(2,1)S(1)}, bf16[8,56,1,8,72]{4,3,2,1,0:T(8,128)(2,1)}, bf16[8,56,1,8,72]{4,3,2,1,0:T(8,128)(2,1)}) fusion(bf16[8,56,3,8,72]{4,3,2,1,0:T(8,128)(2,1)} %reshape_reshape.6), kind=kLoop, calls=%fused_computation.85 | loop fusion | bytes 3096576 | tf_op jit(solution)/shard_map/slice | solution.py:31
  179.2 3.8 %fusion.46 = (f32[8,8,56]{2,1,0:T(8,128)S(1)}, f32[8,8,56,56]{2,3,1,0:T(8,128)}) fusion(bf16[8,56,1,8,72]{4,3,2,1,0:T(8,128)(2,1)} %get-tuple-element.13, bf16[8,56,1,8,72]{4,3,2,1,0:T(8,128)(2,1)} %get-tuple-element.12), kind=kOutput, calls=%fused_computation.88 | convolution fusion | flops 29503544 | bytes 1849344 | tf_op jit(solution)/shard_map/sub | solution.py:29
  183.0 2.2 %fusion.17 = bf16[8,56,8,72]{3,1,2,0:T(8,128)(2,1)S(1)} fusion(f32[8,8,56,56]{2,3,1,0:T(8,128)} %get-tuple-element.18, bf16[8,56,1,8,72]{4,3,2,1,0:T(8,128)(2,1)S(1)} %get-tuple-element.11, f32[8,8,56]{2,1,0:T(8,128)S(1)} %get-tuple-element.17), kind=kOutput, calls=%fused_computation.39 | convolution fusion | flops 29560832 | bytes 1849344 | tf_op jit(solution)/shard_map/bhqk,bkhs->bqhs/dot_general | solution.py:31
  185.2 0.1 copy.109
  185.3 1.5 reshape_reshape.7
  186.8 0.1 bitcast_convert_fusion
  187.0 0.9 copy-done.1
  187.9 0.4 copy-done.2
  188.3 1.1 fusion.6
  189.4 18.2 %all_to_all.35 = bf16[56,1,8,1152]{3,2,1,0:T(8,128)(2,1)S(1)} all-to-all(bf16[56,1,8,1152]{3,2,1,0:T(8,128)(2,1)S(1)} %fusion.6), channel_id=1, replica_groups=mesh['dp'=32,'seq'=8] {'seq'}, dimensions={0} | all-to-all | bytes 2064384 | tf_op jit(solution)/shard_map/all_to_all | solution.py:83
  207.6 1.1 copy.182
  (24 shorter events, 0.3 us)
Async XLA Ops:
  0.0 138.6 %copy-start = (bf16[576,1152]{1,0:T(8,128)(2,1)S(1)}, bf16[576,1152]{1,0:T(8,128)(2,1)}, u32[]{:S(2)}) copy-start(bf16[576,1152]{1,0:T(8,128)(2,1)} %param.13) | copy-start | bytes 3981316
  6.7 12.2 %copy-start.4 = (s32[32,13]{0,1:T(8,128)S(1)}, s32[32,13]{0,1:T(8,128)}, u32[]{:S(2)}) copy-start(s32[32,13]{0,1:T(8,128)} %param.11) | copy-start | bytes 4996
  6.7 12.2 %copy-start.5 = (s32[32]{0:T(128)S(1)}, s32[32]{0:T(128)}, u32[]{:S(2)}) copy-start(s32[32]{0:T(128)} %param.10) | copy-start | bytes 388
  6.7 57.0 %all-to-all-start = ((bf16[32,13,2,1152]{3,2,1,0:T(2,128)(2,1)}), bf16[32,13,2,1152]{3,2,1,0:T(2,128)(2,1)S(1)}, u32[]{:S(2)}, u32[]{:S(2)}) async-start(bf16[32,13,2,1152]{3,2,1,0:T(2,128)(2,1)} %bitcast.114), calls=%async_computation | async-start | bytes 3833856 | tf_op jit(solution)/shard_map/all_to_all | solution.py:60
  67.4 9.4 %copy-start.3 = (f32[1,6,1152]{2,0,1:T(1,128)S(1)}, f32[1,6,1152]{2,0,1:T(1,128)}, u32[]{:S(2)}) copy-start(f32[1,6,1152]{2,0,1:T(1,128)} %param.9) | copy-start | bytes 82948
  70.4 31.1 %all-to-all-start.1 = ((bf16[32,7,2,1152]{3,2,1,0:T(2,128)(2,1)}), bf16[32,7,2,1152]{3,2,1,0:T(2,128)(2,1)S(1)}, u32[]{:S(2)}, u32[]{:S(2)}) async-start(bf16[32,7,2,1152]{3,2,1,0:T(2,128)(2,1)} %broadcast_select_fusion), calls=%async_computation.1 | async-start | bytes 2064384 | tf_op jit(solution)/shard_map/all_to_all | solution.py:62
  186.8 1.1 copy-start.1
  186.8 1.5 copy-start.2

commit v2 on v1

v2 whole, which is shorter than its diff:
```python
import functools
import math

import jax
import jax.numpy as jnp
from jax import lax
from jax.experimental import pallas as pl
from jax.experimental.pallas import tpu as pltpu
from jax.sharding import PartitionSpec as P

HEADS = 8
HEAD_DIM = 72
HD = HEADS * HEAD_DIM
SECTION = 640
NFD = 7
EPS = 1e-06
LOW = -1e30
NT = (((1,), (1,)), ((), ()))


def block_kernel(groups, x_ref, mod_ref, w_ref, wo_ref, rows_ref, cols_ref, o_ref, qkv_ref, s_ref, p_ref, mix_ref):
    values = x_ref[...].astype(jnp.float32)
    center = values - jnp.mean(values, axis=-1, keepdims=True)
    spread = jnp.mean(center * center, axis=-1, keepdims=True)
    normed = center * lax.rsqrt(spread + EPS) * (1.0 + mod_ref[1:2, :]) + mod_ref[0:1, :]
    normed = normed.astype(jnp.bfloat16)
    for part in range(3):
        start = part * SECTION
        qkv_ref[:, start + SECTION - 128 : start + SECTION] = jnp.zeros((values.shape[0], 128), jnp.bfloat16)
        qkv_ref[:, start : start + HD] = lax.dot_general(
            normed, w_ref[part * HD : (part + 1) * HD, :], NT, preferred_element_type=jnp.float32
        ).astype(jnp.bfloat16)
    mix_ref[...] = jnp.zeros_like(mix_ref)
    factor = 1.0 / math.sqrt(HEAD_DIM)
    lane = lax.broadcasted_iota(jnp.int32, (1, 256), 1)
    tasks = [(h, start, size) for start, size in groups for h in range(HEADS)]

    def window(h):
        base = (HEAD_DIM * h) // 128 * 128
        low = HEAD_DIM * h - base
        return base, (lane >= low) & (lane < low + HEAD_DIM)

    def scores(t):
        h, start, size = tasks[t]
        base, own = window(h)
        rows = pl.ds(start, size)
        q = jnp.where(own, qkv_ref[rows, pl.ds(base, 256)], jnp.bfloat16(0))
        k = qkv_ref[rows, pl.ds(SECTION + base, 256)]
        s_ref[t % 2, :size, :size] = lax.dot_general(q, k, NT, preferred_element_type=jnp.float32)

    def weights(t):
        h, start, size = tasks[t]
        same = rows_ref[start : start + size, 0:1] == cols_ref[0:1, start : start + size]
        s = jnp.where(same, s_ref[t % 2, :size, :size] * factor, LOW)
        raised = jnp.exp(s - jnp.max(s, axis=-1, keepdims=True))
        p_ref[t % 2, :size, :size] = (raised / jnp.sum(raised, axis=-1, keepdims=True)).astype(jnp.bfloat16)

    def mixing(t):
        h, start, size = tasks[t]
        base, own = window(h)
        rows = pl.ds(start, size)
        mixed = jnp.dot(
            p_ref[t % 2, :size, :size],
            qkv_ref[rows, pl.ds(2 * SECTION + base, 256)],
            preferred_element_type=jnp.float32,
        ).astype(jnp.bfloat16)
        mix_ref[rows, pl.ds(base, 256)] = jnp.where(own, mixed, mix_ref[rows, pl.ds(base, 256)])

    scores(0)
    for t in range(len(tasks)):
        if t + 1 < len(tasks):
            scores(t + 1)
        weights(t)
        mixing(t)
    projected = jnp.dot(mix_ref[:, 0:HD], wo_ref[...], preferred_element_type=jnp.float32)
    o_ref[...] = (x_ref[...].astype(jnp.float32) + mod_ref[2:3, :] * projected).astype(jnp.bfloat16)


def block(x, mod, w_qkv, w_out, ids, groups):
    rows, width = x.shape
    biggest = max(size for _, size in groups)
    vmem = pl.BlockSpec(memory_space=pltpu.VMEM)
    return pl.pallas_call(
        functools.partial(block_kernel, groups),
        out_shape=jax.ShapeDtypeStruct(x.shape, x.dtype),
        in_specs=[vmem] * 6,
        out_specs=vmem,
        scratch_shapes=[
            pltpu.VMEM((rows, 3 * SECTION), jnp.bfloat16),
            pltpu.VMEM((2, biggest, biggest), jnp.float32),
            pltpu.VMEM((2, biggest, biggest), jnp.bfloat16),
            pltpu.VMEM((rows, SECTION), jnp.bfloat16),
        ],
        compiler_params=pltpu.CompilerParams(vmem_limit_bytes=26 * 1024 * 1024),
        cost_estimate=pl.CostEstimate(
            flops=2 * rows * width * (3 * SECTION + SECTION) + 4 * HEADS * rows * biggest * 256,
            bytes_accessed=2 * 2 * rows * width + 2 * 4 * SECTION * width,
            transcendentals=HEADS * rows * biggest,
        ),
    )(x, mod, w_qkv, w_out, ids.reshape(-1, 1), ids.reshape(1, -1))


def source_index(counts, dest):
    groups, slots = dest.shape
    slot_ids = jnp.arange(slots, dtype=jnp.int32)
    live = slot_ids[None, :] < counts[:, None]
    targets = jnp.where(live, dest, -1).reshape(-1)
    wanted = jnp.arange(groups * NFD, dtype=jnp.int32)
    anchors = jnp.arange(groups * slots, dtype=jnp.int32)
    return jnp.sum(jnp.where(targets[None, :] == wanted[:, None], anchors[None, :], 0), axis=1)


def on_device(slot_tokens, modulation, counts, dest, qkv_spatial, out_spatial, qkv_temporal, out_temporal):
    groups = lax.axis_size("dp")
    shards = lax.axis_size("seq")
    slots, patches, width = slot_tokens.shape
    piece = patches // groups
    mod = modulation[0]
    pieces = slot_tokens.reshape(slots, groups, piece, width).transpose(1, 0, 2, 3)
    spread = lax.all_to_all(pieces, "dp", split_axis=0, concat_axis=0, tiled=True)
    chosen = jnp.take(
        spread.reshape(groups * slots, piece, width), source_index(counts, dest), axis=0, mode="clip"
    )
    gathered = lax.all_to_all(
        chosen.reshape(groups, NFD, piece, width), "dp", split_axis=0, concat_axis=0, tiled=True
    )
    frames = gathered.transpose(1, 0, 2, 3).reshape(NFD * patches, width)
    row = jnp.arange(NFD * patches, dtype=jnp.int32)
    after = block(
        frames,
        mod[0:3],
        qkv_spatial.T,
        out_spatial,
        row // patches,
        ((0, 4 * patches), (4 * patches, 3 * patches)),
    )
    widest = patches // shards
    total = shards * NFD
    moved = lax.all_to_all(
        after.reshape(NFD, shards, widest, width), "seq", split_axis=1, concat_axis=0, tiled=True
    )
    home = block(
        moved.reshape(total * widest, width),
        mod[3:6],
        qkv_temporal.T,
        out_temporal,
        row % widest,
        ((0, total * widest),),
    )
    back = lax.all_to_all(
        home.reshape(total, 1, widest, width), "seq", split_axis=0, concat_axis=1, tiled=True
    )
    return back.reshape(NFD, patches, width)


def solution(mesh):
    in_specs = (P("dp", "seq", None), P("dp", None, None), P(), P(), P(), P(), P(), P())
    return jax.shard_map(
        on_device, mesh=mesh, in_specs=in_specs, out_specs=P("dp", "seq", None), check_vma=False
    )
```

time: 210 us -> 165 us (0.79)
  matrix products: 28.4 us -> 0 us
  local copies, waits for them, and re-layouts: 44.2 us -> 21.3 us
  blocking collectives: 40.8 us -> 18.2 us
  waiting for transfers between devices: 68.9 us -> 83.8 us
  Pallas kernels: 0 us -> 14.8 us
  starting transfers between devices: 18.5 us -> 26.6 us
  other arithmetic: 7.6 us -> 0.21 us
    all_to_all x1 -> x0, blocking collectives: 22.6 us -> none  [on_device(): lax.all_to_all(after.reshape(NFD, shards, widest, width), 'seq', split_ax...]
    dot_general x7 -> x0, matrix products: 22.3 us -> none  [the longest x2 10.1 us: block(): jnp.dot(normed, w_qkv, preferred_element_type=jnp.float32)]
    pallas_call x0 -> x2, Pallas kernels: none -> 14.8 us  [block(): pl.pallas_call(functools.partial(block_kernel, groups), out_shape=jax.Sha...]
    all_to_all x0 -> x1, waiting for transfers between devices: none -> 14.7 us  [on_device(): lax.all_to_all(after.reshape(NFD, shards, widest, width), 'seq', split_ax...]
    all_to_all x0 -> x1, starting transfers between devices: none -> 8.04 us  [on_device(): lax.all_to_all(after.reshape(NFD, shards, widest, width), 'seq', split_ax...]
    convert_element_type x4 -> x0, local copies, waits for them, and re-layouts: 7.57 us -> none  [the longest x2 4.74 us: block(): return (rows.astype(jnp.float32) + gate * projected).astype(jnp.bfloat16)]
    another operation x2 -> x0, local copies, waits for them, and re-layouts: 6.92 us -> none  [the longest x1 5.41 us: attention(): parts = qkv_rows.reshape(batch_count, length, 3, HEADS, HEAD_DIM)]
    reshape x3 -> x1, local copies, waits for them, and re-layouts: 9.41 us -> 2.62 us  [on_device(): frames = gathered.transpose(1, 0, 2, 3).reshape(NFD * patches, width)]
  transfers between devices with their start and end apart: 2 -> 3, of which waited for: 2 -> 3; matrix products, arithmetic and copies ran while one was open for 0% -> 0% of each run, Pallas kernels for 0% -> 0%
where the time goes in v2:
time: 165 us
  waiting for transfers between devices  83.8 us (51%)
  starting transfers between devices  26.6 us (16%)
  local copies, waits for them, and re-layouts  21.3 us (13%)
  blocking collectives  18.2 us (11%)
  Pallas kernels  14.8 us (9%)
    all_to_all x1, waiting for transfers between devices, on_device(): lax.all_to_all(pieces, 'dp', split_axis=0, concat_axis=0, tiled=True)  44.4 us
    all_to_all x1, waiting for transfers between devices, on_device(): lax.all_to_all(chosen.reshape(groups, NFD, piece, width), 'dp', split_axi...  24.6 us
    all_to_all x1, blocking collectives, on_device(): lax.all_to_all(home.reshape(total, 1, widest, width), 'seq', split_axis=0...  18.2 us
    pallas_call x2, Pallas kernels, block(): pl.pallas_call(functools.partial(block_kernel, groups), out_shape=jax.Sha...  14.8 us
    all_to_all x1, waiting for transfers between devices, on_device(): lax.all_to_all(after.reshape(NFD, shards, widest, width), 'seq', split_ax...  14.7 us
    all_to_all x1, starting transfers between devices, on_device(): lax.all_to_all(pieces, 'dp', split_axis=0, concat_axis=0, tiled=True)  12.2 us
    all_to_all x1, starting transfers between devices, on_device(): lax.all_to_all(after.reshape(NFD, shards, widest, width), 'seq', split_ax...  8.04 us
    reshape x2, local copies, waits for them, and re-layouts, on_device(): slot_tokens.reshape(slots, groups, piece, width).transpose(1, 0, 2, 3)  6.62 us
  transfers between devices with their start and end apart: 3, of which 3 were waited for; matrix products, arithmetic and copies ran while one was open for 0% of the time, Pallas kernels for 0%

profile of v2, /device:TPU:1, one launch (start us, length us, event | category | flops | bytes accessed | tf_op | source)
XLA Modules:
  0.0 165.0 jit_solution(17287279384660391600)
XLA Ops:
  0.0 4.0 %reshape.146 = bf16[13,32,2,1152]{3,2,1,0:T(2,128)(2,1)S(1)} reshape(bf16[13,64,1152]{2,1,0:T(8,128)(2,1)} %param.8) | data formatting | bytes 3833856 | tf_op jit(solution)/shard_map/reshape | solution.py:119
  4.0 2.6 %copy.42 = bf16[13,32,2,1152]{3,2,0,1:T(2,128)(2,1)} copy(bf16[13,32,2,1152]{3,2,1,0:T(2,128)(2,1)S(1)} %reshape.146) | data formatting | bytes 3833856 | tf_op jit(solution)/shard_map/reshape | solution.py:119
  6.6 0.0 copy-start.5
  6.6 0.0 copy-start.6
  6.6 12.2 %all-to-all-start = ((bf16[32,13,2,1152]{3,2,1,0:T(2,128)(2,1)}), bf16[32,13,2,1152]{3,2,1,0:T(2,128)(2,1)S(1)}, u32[]{:S(2)}, u32[]{:S(2)}) async-start(bf16[32,13,2,1152]{3,2,1,0:T(2,128)(2,1)} %bitcast.25), calls=%async_computation | async-start | bytes 3833856 | tf_op jit(solution)/shard_map/all_to_all | solution.py:120
  18.8 0.0 copy-done.5
  18.8 0.0 copy-done.6
  18.8 0.1 copy.29
  18.9 0.1 eq.17
  19.0 0.1 select_reduce_fusion
  19.2 44.4 %all-to-all-done = bf16[32,13,2,1152]{3,2,1,0:T(2,128)(2,1)S(1)} async-done(((bf16[32,13,2,1152]{3,2,1,0:T(2,128)(2,1)}), bf16[32,13,2,1152]{3,2,1,0:T(2,128)(2,1)S(1)}, u32[]{:S(2)}, u32[]{:S(2)}) %all-to-all-start) | async-done | bytes 1916960 | tf_op jit(solution)/shard_map/all_to_all | solution.py:120
  63.6 0.0 copy-start.4
  63.6 3.7 %gather_fusion = bf16[224,2,1152]{2,1,0:T(2,128)(2,1)} fusion(bf16[416,2,1152]{2,1,0:T(2,128)(2,1)S(1)} %bitcast.36, s32[1024]{0:T(1024)S(1)} %pad_clamp_fusion), kind=kCustom, calls=%fused_computation | custom fusion | bytes 2065280 | tf_op jit(solution)/shard_map/jit(_take)/gather | solution.py:121
  67.3 6.4 %all-to-all-start.1 = ((bf16[32,7,2,1152]{3,2,1,0:T(2,128)(2,1)}), bf16[32,7,2,1152]{3,2,1,0:T(2,128)(2,1)S(1)}, u32[]{:S(2)}, u32[]{:S(2)}) async-start(bf16[32,7,2,1152]{3,2,1,0:T(2,128)(2,1)} %bitcast.2), calls=%async_computation.1 | async-start | bytes 2064384 | tf_op jit(solution)/shard_map/all_to_all | solution.py:124
  73.7 0.0 copy-done.4
  73.8 24.6 %all-to-all-done.1 = bf16[32,7,2,1152]{3,2,1,0:T(2,128)(2,1)S(1)} async-done(((bf16[32,7,2,1152]{3,2,1,0:T(2,128)(2,1)}), bf16[32,7,2,1152]{3,2,1,0:T(2,128)(2,1)S(1)}, u32[]{:S(2)}, u32[]{:S(2)}) %all-to-all-start.1) | async-done | bytes 1032224 | tf_op jit(solution)/shard_map/all_to_all | solution.py:124
  98.4 0.0 copy-start.2
  98.4 1.7 %copy.30 = bf16[7,32,2,1152]{3,2,1,0:T(2,128)(2,1)} copy(bf16[7,32,2,1152]{3,2,0,1:T(2,128)(2,1)S(1)} %bitcast.37) | data formatting | bytes 2064384 | tf_op jit(solution)/shard_map/transpose | solution.py:127
  100.1 2.6 %reshape.149.x_ref = bf16[448,1152]{1,0:T(8,128)(2,1)S(1)} reshape(bf16[7,32,2,1152]{3,2,1,0:T(2,128)(2,1)} %copy.30) | data formatting | bytes 2064384 | tf_op jit(solution)/shard_map/reshape | solution.py:127
  102.8 0.0 copy-done.2
  102.8 0.0 copy-start
  102.8 2.1 %copy-done = bf16[1152,1728]{0,1:T(8,128)(2,1)S(1)} copy-done((bf16[1152,1728]{0,1:T(8,128)(2,1)S(1)}, bf16[1152,1728]{0,1:T(8,128)(2,1)}, u32[]{:S(2)}) %copy-start) | copy-done | bytes 3981336
  104.9 6.9 %shard_map.82 = bf16[448,1152]{1,0:T(8,128)(2,1)S(1)} custom-call(bf16[448,1152]{1,0:T(8,128)(2,1)S(1)} %reshape.149.x_ref, f32[3,1152]{1,0:T(4,128)S(1)} %bitcast.32, bf16[1728,1152]{1,0:T(8,128)(2,1)S(1)} %bitcast.34, bf16[576,1152]{1,0:T(8,128)(2,1)S(1)} %copy-done.2, s32[448,1]{1,0:T(8,128)S(1)} %add_select_fusion.1.rows_ref, ...), custom_call_target="tpu_custom_call" | custom-call | flops 3581935616 | bytes 7962624 | tf_op jit(solution)/shard_map/pallas_call | solution.py:83
  111.8 0.0 copy-start.3
  111.8 1.0 copy.32
  112.8 8.0 %all-to-all-start.2 = ((bf16[7,8,8,1152]{3,2,0,1:T(8,128)(2,1)}), bf16[7,8,8,1152]{3,2,0,1:T(8,128)(2,1)S(1)}, u32[]{:S(2)}, u32[]{:S(2)}) async-start(bf16[7,8,8,1152]{3,2,0,1:T(8,128)(2,1)} %copy.32), calls=%async_computation.2 | async-start | bytes 2064384 | tf_op jit(solution)/shard_map/all_to_all | solution.py:139
  120.9 14.7 %all-to-all-done.2 = bf16[7,8,8,1152]{3,2,0,1:T(8,128)(2,1)S(1)} async-done(((bf16[7,8,8,1152]{3,2,0,1:T(8,128)(2,1)}), bf16[7,8,8,1152]{3,2,0,1:T(8,128)(2,1)S(1)}, u32[]{:S(2)}, u32[]{:S(2)}) %all-to-all-start.2) | async-done | bytes 1032224 | tf_op jit(solution)/shard_map/all_to_all | solution.py:139
  135.6 0.0 copy-done.3
  135.7 0.0 copy-start.1
  135.7 2.1 %copy-done.1 = bf16[1152,1728]{0,1:T(8,128)(2,1)S(1)} copy-done((bf16[1152,1728]{0,1:T(8,128)(2,1)S(1)}, bf16[1152,1728]{0,1:T(8,128)(2,1)}, u32[]{:S(2)}) %copy-start.1) | copy-done | bytes 3981336
  137.8 7.9 %shard_map.83 = bf16[448,1152]{1,0:T(8,128)(2,1)S(1)} custom-call(bf16[448,1152]{1,0:T(8,128)(2,1)S(1)} %bitcast.29, f32[3,1152]{1,0:T(4,128)S(1)} %bitcast.33, bf16[1728,1152]{1,0:T(8,128)(2,1)S(1)} %bitcast.35, bf16[576,1152]{1,0:T(8,128)(2,1)S(1)} %copy-done.3, s32[448,1]{1,0:T(8,128)S(1)} %add_select_fusion.rows_ref, s32[1,448]{1,0:T(1,128)S(1)} %and_select_fusion.cols_ref), custom_call_target="tpu_custom_call" | custom-call | flops 4286578688 | bytes 7962624 | tf_op jit(solution)/shard_map/pallas_call | solution.py:83
  145.7 18.2 %all_to_all.40 = bf16[56,1,8,1152]{3,2,1,0:T(8,128)(2,1)S(1)} all-to-all(bf16[56,1,8,1152]{3,2,1,0:T(8,128)(2,1)S(1)} %bitcast.31), channel_id=1, replica_groups=mesh['dp'=32,'seq'=8] {'seq'}, dimensions={0} | all-to-all | bytes 2064384 | tf_op jit(solution)/shard_map/all_to_all | solution.py:150
  163.9 1.1 copy.43
  (9 shorter events, 0.1 us)
Async XLA Ops:
  6.6 12.2 %copy-start.5 = (s32[32,13]{0,1:T(8,128)S(1)}, s32[32,13]{0,1:T(8,128)}, u32[]{:S(2)}) copy-start(s32[32,13]{0,1:T(8,128)} %param.11) | copy-start | bytes 4996
  6.6 12.2 %copy-start.6 = (s32[32]{0:T(128)S(1)}, s32[32]{0:T(128)}, u32[]{:S(2)}) copy-start(s32[32]{0:T(128)} %param.10) | copy-start | bytes 388
  6.6 57.0 %all-to-all-start = ((bf16[32,13,2,1152]{3,2,1,0:T(2,128)(2,1)}), bf16[32,13,2,1152]{3,2,1,0:T(2,128)(2,1)S(1)}, u32[]{:S(2)}, u32[]{:S(2)}) async-start(bf16[32,13,2,1152]{3,2,1,0:T(2,128)(2,1)} %bitcast.25), calls=%async_computation | async-start | bytes 3833856 | tf_op jit(solution)/shard_map/all_to_all | solution.py:120
  63.6 10.1 %copy-start.4 = (f32[1,6,1152]{2,0,1:T(1,128)S(1)}, f32[1,6,1152]{2,0,1:T(1,128)}, u32[]{:S(2)}) copy-start(f32[1,6,1152]{2,0,1:T(1,128)} %param.9) | copy-start | bytes 82948
  67.3 31.1 %all-to-all-start.1 = ((bf16[32,7,2,1152]{3,2,1,0:T(2,128)(2,1)}), bf16[32,7,2,1152]{3,2,1,0:T(2,128)(2,1)S(1)}, u32[]{:S(2)}, u32[]{:S(2)}) async-start(bf16[32,7,2,1152]{3,2,1,0:T(2,128)(2,1)} %bitcast.2), calls=%async_computation.1 | async-start | bytes 2064384 | tf_op jit(solution)/shard_map/all_to_all | solution.py:124
  98.4 4.3 %copy-start.2 = (bf16[576,1152]{1,0:T(8,128)(2,1)S(1)}, bf16[576,1152]{1,0:T(8,128)(2,1)}, u32[]{:S(2)}) copy-start(bf16[576,1152]{1,0:T(8,128)(2,1)} %wo_ref.2) | copy-start | bytes 3981316
  102.8 2.1 %copy-start = (bf16[1152,1728]{0,1:T(8,128)(2,1)S(1)}, bf16[1152,1728]{0,1:T(8,128)(2,1)}, u32[]{:S(2)}) copy-start(bf16[1152,1728]{0,1:T(8,128)(2,1)} %param.12) | copy-start | bytes 11943940
  111.8 23.9 %copy-start.3 = (bf16[576,1152]{1,0:T(8,128)(2,1)S(1)}, bf16[576,1152]{1,0:T(8,128)(2,1)}, u32[]{:S(2)}) copy-start(bf16[576,1152]{1,0:T(8,128)(2,1)} %wo_ref.3) | copy-start | bytes 3981316
  112.8 22.8 %all-to-all-start.2 = ((bf16[7,8,8,1152]{3,2,0,1:T(8,128)(2,1)}), bf16[7,8,8,1152]{3,2,0,1:T(8,128)(2,1)S(1)}, u32[]{:S(2)}, u32[]{:S(2)}) async-start(bf16[7,8,8,1152]{3,2,0,1:T(8,128)(2,1)} %copy.32), calls=%async_computation.2 | async-start | bytes 2064384 | tf_op jit(solution)/shard_map/all_to_all | solution.py:139
  135.7 2.1 %copy-start.1 = (bf16[1152,1728]{0,1:T(8,128)(2,1)S(1)}, bf16[1152,1728]{0,1:T(8,128)(2,1)}, u32[]{:S(2)}) copy-start(bf16[1152,1728]{0,1:T(8,128)(2,1)} %param.14) | copy-start | bytes 11943940

commit v3 on v2

v3 whole, which is shorter than its diff:
```python
import functools
import math

import jax
import jax.numpy as jnp
from jax import lax
from jax.experimental import pallas as pl
from jax.experimental.pallas import tpu as pltpu
from jax.sharding import PartitionSpec as P

HEADS = 8
HEAD_DIM = 72
HD = HEADS * HEAD_DIM
SECTION = 640
NFD = 7
EPS = 1e-06
LOW = -1e30
NT = (((1,), (1,)), ((), ()))
VMEM = pl.BlockSpec(memory_space=pltpu.VMEM)
HBM = pl.BlockSpec(memory_space=pltpu.HBM)
SMEM = pl.BlockSpec(memory_space=pltpu.SMEM)


def limit(mib):
    return pltpu.CompilerParams(vmem_limit_bytes=mib * 1024 * 1024)


def spread_kernel(x_ref, o_ref):
    slots = x_ref.shape[0]
    for q in range(slots):
        o_ref[:, q] = x_ref[q].reshape(o_ref.shape[0], 2, x_ref.shape[2])


def spread_pieces(slot_tokens, groups):
    slots, patches, width = slot_tokens.shape
    steps = 4
    return pl.pallas_call(
        spread_kernel,
        out_shape=jax.ShapeDtypeStruct((groups, slots, 2, width), slot_tokens.dtype),
        grid=(steps,),
        in_specs=[pl.BlockSpec((slots, patches // steps, width), lambda i: (0, i, 0))],
        out_specs=pl.BlockSpec((groups // steps, slots, 2, width), lambda i: (i, 0, 0, 0)),
        compiler_params=limit(63),
    )(slot_tokens)


def choose_kernel(index_ref, x_ref, o_ref):
    unroll = 8

    def body(i, carry):
        for j in range(unroll):
            o_ref[i * unroll + j] = x_ref[index_ref[i * unroll + j]]
        return carry

    lax.fori_loop(0, o_ref.shape[0] // unroll, body, 0)


def choose_pieces(spread, index):
    return pl.pallas_call(
        choose_kernel,
        out_shape=jax.ShapeDtypeStruct((index.shape[0],) + spread.shape[1:], spread.dtype),
        in_specs=[SMEM, VMEM],
        out_specs=VMEM,
        compiler_params=limit(26),
    )(index, spread)


def normalized(values, mod_ref):
    center = values - jnp.mean(values, axis=-1, keepdims=True)
    spread = jnp.mean(center * center, axis=-1, keepdims=True)
    return center * lax.rsqrt(spread + EPS) * (1.0 + mod_ref[1:2, :]) + mod_ref[0:1, :]


def project_qkv(normed, w_ref, waits, qkv_ref):
    for part in range(3):
        start = part * SECTION
        qkv_ref[:, start + SECTION - 128 : start + SECTION] = jnp.zeros((normed.shape[0], 128), jnp.bfloat16)
        waits[part].wait()
        qkv_ref[:, start : start + HD] = lax.dot_general(
            normed, w_ref[part * HD : (part + 1) * HD, :], NT, preferred_element_type=jnp.float32
        ).astype(jnp.bfloat16)


def attend(groups, rows_ref, cols_ref, qkv_ref, s_ref, p_ref, mix_ref):
    factor = 1.0 / math.sqrt(HEAD_DIM)
    lane = lax.broadcasted_iota(jnp.int32, (1, 256), 1)
    tasks = [(h, start, size) for start, size in groups for h in range(HEADS)]

    def window(h):
        base = (HEAD_DIM * h) // 128 * 128
        low = HEAD_DIM * h - base
        return base, (lane >= low) & (lane < low + HEAD_DIM)

    def scores(t):
        h, start, size = tasks[t]
        base, own = window(h)
        rows = pl.ds(start, size)
        q = jnp.where(own, qkv_ref[rows, pl.ds(base, 256)], jnp.bfloat16(0))
        k = qkv_ref[rows, pl.ds(SECTION + base, 256)]
        s_ref[t % 2, :size, :size] = lax.dot_general(q, k, NT, preferred_element_type=jnp.float32)

    def weights(t):
        h, start, size = tasks[t]
        same = rows_ref[start : start + size, 0:1] == cols_ref[0:1, start : start + size]
        s = jnp.where(same, s_ref[t % 2, :size, :size] * factor, LOW)
        raised = jnp.exp(s - jnp.max(s, axis=-1, keepdims=True))
        p_ref[t % 2, :size, :size] = (raised / jnp.sum(raised, axis=-1, keepdims=True)).astype(jnp.bfloat16)

    def mixing(t):
        h, start, size = tasks[t]
        base, own = window(h)
        rows = pl.ds(start, size)
        mixed = jnp.dot(
            p_ref[t % 2, :size, :size],
            qkv_ref[rows, pl.ds(2 * SECTION + base, 256)],
            preferred_element_type=jnp.float32,
        ).astype(jnp.bfloat16)
        mix_ref[rows, pl.ds(base, 256)] = jnp.where(own, mixed, mix_ref[rows, pl.ds(base, 256)])

    scores(0)
    for t in range(len(tasks)):
        if t + 1 < len(tasks):
            scores(t + 1)
        weights(t)
        mixing(t)


def fetch_qkv(w_hbm, w_ref, sems):
    copies = [
        pltpu.make_async_copy(
            w_hbm.at[pl.ds(part * HD, HD)], w_ref.at[pl.ds(part * HD, HD)], sems.at[part]
        )
        for part in range(3)
    ]
    for copy in copies:
        copy.start()
    return copies


def spatial_kernel(
    groups, x_ref, mod_ref, w_hbm, wo_hbm, rows_ref, cols_ref, o_ref,
    frames_ref, w_ref, wo_ref, qkv_ref, s_ref, p_ref, mix_ref, sems,
):
    copies = fetch_qkv(w_hbm, w_ref, sems)
    last = pltpu.make_async_copy(wo_hbm, wo_ref, sems.at[3])
    last.start()
    frame_count = x_ref.shape[1]
    patches = frames_ref.shape[0] // frame_count
    for k in range(frame_count):
        frames_ref[k * patches : (k + 1) * patches] = x_ref[:, k].reshape(patches, x_ref.shape[3])
    values = frames_ref[...].astype(jnp.float32)
    project_qkv(normalized(values, mod_ref).astype(jnp.bfloat16), w_ref, copies, qkv_ref)
    mix_ref[...] = jnp.zeros_like(mix_ref)
    attend(groups, rows_ref, cols_ref, qkv_ref, s_ref, p_ref, mix_ref)
    last.wait()
    shards = o_ref.shape[0]
    widest = patches // shards
    for k in range(frame_count):
        rows = pl.ds(k * patches, patches)
        projected = jnp.dot(mix_ref[rows, 0:HD], wo_ref[...], preferred_element_type=jnp.float32)
        after = frames_ref[rows, :].astype(jnp.float32) + mod_ref[2:3, :] * projected
        for j in range(shards):
            o_ref[j, k * widest : (k + 1) * widest, :] = after[j * widest : (j + 1) * widest].astype(jnp.bfloat16)


def spatial_block(gathered, mod, w_qkv, w_out, ids, groups, shards):
    pieces, frame_count, piece, width = gathered.shape
    rows = pieces * frame_count * piece
    biggest = max(size for _, size in groups)
    return pl.pallas_call(
        functools.partial(spatial_kernel, groups),
        out_shape=jax.ShapeDtypeStruct((shards, rows // shards, width), gathered.dtype),
        in_specs=[VMEM, VMEM, HBM, HBM, VMEM, VMEM],
        out_specs=VMEM,
        scratch_shapes=[
            pltpu.VMEM((rows, width), jnp.bfloat16),
            pltpu.VMEM(w_qkv.shape, jnp.bfloat16),
            pltpu.VMEM(w_out.shape, jnp.bfloat16),
            pltpu.VMEM((rows, 3 * SECTION), jnp.bfloat16),
            pltpu.VMEM((2, biggest, biggest), jnp.float32),
            pltpu.VMEM((2, biggest, biggest), jnp.bfloat16),
            pltpu.VMEM((rows, SECTION), jnp.bfloat16),
            pltpu.SemaphoreType.DMA((4,)),
        ],
        compiler_params=limit(51),
    )(gathered, mod, w_qkv, w_out, ids.reshape(-1, 1), ids.reshape(1, -1))


def temporal_kernel(
    groups, x_ref, mod_ref, w_hbm, rows_ref, cols_ref, o_ref, w_ref, qkv_ref, s_ref, p_ref, mix_ref, sems
):
    copies = fetch_qkv(w_hbm, w_ref, sems)
    values = x_ref[...].astype(jnp.float32)
    project_qkv(normalized(values, mod_ref).astype(jnp.bfloat16), w_ref, copies, qkv_ref)
    mix_ref[...] = jnp.zeros_like(mix_ref)
    attend(groups, rows_ref, cols_ref, qkv_ref, s_ref, p_ref, mix_ref)
    o_ref[...] = mix_ref[:, 0:HD]


def temporal_block(x, mod, w_qkv, ids, groups):
    rows, width = x.shape
    biggest = max(size for _, size in groups)
    return pl.pallas_call(
        functools.partial(temporal_kernel, groups),
        out_shape=jax.ShapeDtypeStruct((rows, HD), x.dtype),
        in_specs=[VMEM, VMEM, HBM, VMEM, VMEM],
        out_specs=VMEM,
        scratch_shapes=[
            pltpu.VMEM(w_qkv.shape, jnp.bfloat16),
            pltpu.VMEM((rows, 3 * SECTION), jnp.bfloat16),
            pltpu.VMEM((2, biggest, biggest), jnp.float32),
            pltpu.VMEM((2, biggest, biggest), jnp.bfloat16),
            pltpu.VMEM((rows, SECTION), jnp.bfloat16),
            pltpu.SemaphoreType.DMA((3,)),
        ],
        compiler_params=limit(52),
    )(x, mod, w_qkv, ids.reshape(-1, 1), ids.reshape(1, -1))


def final_kernel(mixed_ref, after_ref, mod_ref, wo_ref, o_ref):
    frame_count, patches, _ = o_ref.shape
    shards = after_ref.shape[0]
    widest = patches // shards
    for j in range(shards):
        projected = jnp.dot(mixed_ref[j], wo_ref[...], preferred_element_type=jnp.float32)
        result = after_ref[j].astype(jnp.float32) + mod_ref[2:3, :] * projected
        for k in range(frame_count):
            o_ref[k, j * widest : (j + 1) * widest, :] = result[k * widest : (k + 1) * widest].astype(jnp.bfloat16)


def final_block(mixed, after, mod, w_out):
    shards, rows, width = after.shape
    return pl.pallas_call(
        final_kernel,
        out_shape=jax.ShapeDtypeStruct((NFD, shards * rows // NFD, width), after.dtype),
        in_specs=[VMEM] * 4,
        out_specs=VMEM,
        compiler_params=limit(26),
    )(mixed, after, mod, w_out)


def source_index(counts, dest):
    groups, slots = dest.shape
    slot_ids = jnp.arange(slots, dtype=jnp.int32)
    live = slot_ids[None, :] < counts[:, None]
    targets = jnp.where(live, dest, -1).reshape(-1)
    wanted = jnp.arange(groups * NFD, dtype=jnp.int32)
    anchors = jnp.arange(groups * slots, dtype=jnp.int32)
    return jnp.sum(jnp.where(targets[None, :] == wanted[:, None], anchors[None, :], 0), axis=1)


def on_device(slot_tokens, modulation, counts, dest, qkv_spatial, out_spatial, qkv_temporal, out_temporal):
    groups = lax.axis_size("dp")
    shards = lax.axis_size("seq")
    slots, patches, width = slot_tokens.shape
    piece = patches // groups
    mod = modulation[0]
    spread = lax.all_to_all(spread_pieces(slot_tokens, groups), "dp", split_axis=0, concat_axis=0, tiled=True)
    chosen = choose_pieces(spread.reshape(groups * slots, piece, width), source_index(counts, dest))
    gathered = lax.all_to_all(
        chosen.reshape(groups, NFD, piece, width), "dp", split_axis=0, concat_axis=0, tiled=True
    )
    row = jnp.arange(NFD * patches, dtype=jnp.int32)
    after = spatial_block(
        gathered,
        mod[0:3],
        qkv_spatial.T,
        out_spatial,
        row // patches,
        ((0, 4 * patches), (4 * patches, 3 * patches)),
        shards,
    )
    widest = patches // shards
    moved = lax.all_to_all(after, "seq", split_axis=0, concat_axis=0, tiled=True)
    mixed = temporal_block(
        moved.reshape(NFD * patches, width), mod[3:6], qkv_temporal.T, row % widest, ((0, NFD * patches),)
    )
    back = lax.all_to_all(
        mixed.reshape(shards, NFD * widest, HD), "seq", split_axis=0, concat_axis=0, tiled=True
    )
    return final_block(back, after, mod[3:6], out_temporal)


def solution(mesh):
    in_specs = (P("dp", "seq", None), P("dp", None, None), P(), P(), P(), P(), P(), P())
    return jax.shard_map(
        on_device, mesh=mesh, in_specs=in_specs, out_specs=P("dp", "seq", None), check_vma=False
    )
```

time: 165 us -> 153 us (0.927)
  local copies, waits for them, and re-layouts: 21.3 us -> 0.22 us
  Pallas kernels: 14.8 us -> 28.5 us
  blocking collectives: 18.2 us -> 13.6 us
    pallas_call x2 -> x5, Pallas kernels: 14.8 us -> 28.5 us  [the longest x1 9.79 us: spatial_block(): pl.pallas_call(functools.partial(spatial_kernel, groups), out_shape=jax.S...]
    reshape x4 -> x0, local copies, waits for them, and re-layouts: 10.3 us -> none  [the longest x2 6.62 us: on_device(): slot_tokens.reshape(slots, groups, piece, width).transpose(1, 0, 2, 3)]
    all_to_all x1, blocking collectives: 18.2 us -> 13.6 us  [on_device(): lax.all_to_all(mixed.reshape(shards, NFD * widest, HD), 'seq', split_axis...]
    unnamed x16 -> x10, local copies, waits for them, and re-layouts: 4.28 us -> 0.03 us
    gather x1 -> x0, local copies, waits for them, and re-layouts: 3.75 us -> none  [on_device(): jnp.take(spread.reshape(groups * slots, piece, width), source_index(count...]
    transpose x1 -> x0, local copies, waits for them, and re-layouts: 1.67 us -> none  [on_device(): frames = gathered.transpose(1, 0, 2, 3).reshape(NFD * patches, width)]
where the time goes in v3:
time: 153 us
  waiting for transfers between devices  83.9 us (55%)
  Pallas kernels  28.5 us (19%)
  starting transfers between devices  26.5 us (17%)
  blocking collectives  13.6 us (9%)
    all_to_all x1, waiting for transfers between devices, on_device(): lax.all_to_all(spread_pieces(slot_tokens, groups), 'dp', split_axis=0, co...  44.4 us
    all_to_all x1, waiting for transfers between devices, on_device(): lax.all_to_all(chosen.reshape(groups, NFD, piece, width), 'dp', split_axi...  24.7 us
    all_to_all x1, waiting for transfers between devices, on_device(): lax.all_to_all(after, 'seq', split_axis=0, concat_axis=0, tiled=True)  14.7 us
    all_to_all x1, blocking collectives, on_device(): lax.all_to_all(mixed.reshape(shards, NFD * widest, HD), 'seq', split_axis...  13.6 us
    all_to_all x1, starting transfers between devices, on_device(): lax.all_to_all(spread_pieces(slot_tokens, groups), 'dp', split_axis=0, co...  12.2 us
    pallas_call x1, Pallas kernels, spatial_block(): pl.pallas_call(functools.partial(spatial_kernel, groups), out_shape=jax.S...  9.79 us
    pallas_call x1, Pallas kernels, temporal_block(): pl.pallas_call(functools.partial(temporal_kernel, groups), out_shape=jax....  8.8 us
    all_to_all x1, starting transfers between devices, on_device(): lax.all_to_all(after, 'seq', split_axis=0, concat_axis=0, tiled=True)  8.14 us
  transfers between devices with their start and end apart: 3, of which 3 were waited for; matrix products, arithmetic and copies ran while one was open for 0% of the time, Pallas kernels for 0%

profile of v3, /device:TPU:1, one launch (start us, length us, event | category | flops | bytes accessed | tf_op | source)
XLA Modules:
  0.0 153.0 jit_solution(894126335618002903)
XLA Ops:
  0.0 3.8 %shard_map.82 = bf16[32,13,2,1152]{3,2,1,0:T(2,128)(2,1)} custom-call(bf16[13,64,1152]{2,1,0:T(8,128)(2,1)} %x_ref.1), custom_call_target="tpu_custom_call" | custom-call | tf_op jit(solution)/shard_map/pallas_call | solution.py:37
  3.8 0.0 copy-start.2
  3.8 0.0 copy-start.3
  3.8 12.2 %all-to-all-start = ((bf16[32,13,2,1152]{3,2,1,0:T(2,128)(2,1)}), bf16[32,13,2,1152]{3,2,1,0:T(2,128)(2,1)S(1)}, u32[]{:S(2)}, u32[]{:S(2)}) async-start(bf16[32,13,2,1152]{3,2,1,0:T(2,128)(2,1)} %shard_map.82), calls=%async_computation | async-start | bytes 3833856 | tf_op jit(solution)/shard_map/all_to_all | solution.py:258
  16.0 0.0 copy-done.2
  16.0 0.0 copy-done.3
  16.0 0.1 copy.14
  16.1 0.1 eq.17
  16.2 0.1 select_reduce_fusion.index_ref
  16.4 44.4 %all-to-all-done = bf16[32,13,2,1152]{3,2,1,0:T(2,128)(2,1)S(1)} async-done(((bf16[32,13,2,1152]{3,2,1,0:T(2,128)(2,1)}), bf16[32,13,2,1152]{3,2,1,0:T(2,128)(2,1)S(1)}, u32[]{:S(2)}, u32[]{:S(2)}) %all-to-all-start) | async-done | bytes 1916960 | tf_op jit(solution)/shard_map/all_to_all | solution.py:258
  60.8 0.0 copy-start.1
  60.8 1.9 %shard_map.83 = bf16[224,2,1152]{2,1,0:T(2,128)(2,1)} custom-call(s32[224]{0:T(256)S(1)} %select_reduce_fusion.index_ref, bf16[416,2,1152]{2,1,0:T(2,128)(2,1)S(1)} %bitcast.12), custom_call_target="tpu_custom_call" | custom-call | tf_op jit(solution)/shard_map/pallas_call | solution.py:59
  62.7 6.2 %all-to-all-start.1 = ((bf16[32,7,2,1152]{3,2,1,0:T(2,128)(2,1)}), bf16[32,7,2,1152]{3,2,1,0:T(2,128)(2,1)S(1)}, u32[]{:S(2)}, u32[]{:S(2)}) async-start(bf16[32,7,2,1152]{3,2,1,0:T(2,128)(2,1)} %bitcast.1), calls=%async_computation.1 | async-start | bytes 2064384 | tf_op jit(solution)/shard_map/all_to_all | solution.py:260
  68.9 0.0 copy-done.1
  69.0 24.7 %all-to-all-done.1.x_ref = bf16[32,7,2,1152]{3,2,1,0:T(2,128)(2,1)S(1)} async-done(((bf16[32,7,2,1152]{3,2,1,0:T(2,128)(2,1)}), bf16[32,7,2,1152]{3,2,1,0:T(2,128)(2,1)S(1)}, u32[]{:S(2)}, u32[]{:S(2)}) %all-to-all-start.1) | async-done | bytes 1032224 | tf_op jit(solution)/shard_map/all_to_all | solution.py:260
  93.7 9.8 %shard_map.84.after_ref = bf16[8,56,1152]{2,1,0:T(8,128)(2,1)} custom-call(bf16[32,7,2,1152]{3,2,1,0:T(2,128)(2,1)S(1)} %all-to-all-done.1.x_ref, f32[3,1152]{1,0:T(4,128)S(1)} %bitcast.17, bf16[1728,1152]{1,0:T(8,128)(2,1)} %bitcast.18, bf16[576,1152]{1,0:T(8,128)(2,1)} %wo_hbm.1, s32[448,1]{1,0:T(8,128)S(1)} %add_select_fusion.1.rows_ref, ...), custom_call_target="tpu_custom_call" | custom-call | tf_op jit(solution)/shard_map/pallas_call | solution.py:170
  103.5 8.1 %all-to-all-start.2 = ((bf16[8,56,1152]{2,1,0:T(8,128)(2,1)}), bf16[8,56,1152]{2,1,0:T(8,128)(2,1)S(1)}, u32[]{:S(2)}, u32[]{:S(2)}) async-start(bf16[8,56,1152]{2,1,0:T(8,128)(2,1)} %shard_map.84.after_ref), calls=%async_computation.2 | async-start | bytes 2064384 | tf_op jit(solution)/shard_map/all_to_all | solution.py:274
  111.7 14.7 %all-to-all-done.2 = bf16[8,56,1152]{2,1,0:T(8,128)(2,1)S(1)} async-done(((bf16[8,56,1152]{2,1,0:T(8,128)(2,1)}), bf16[8,56,1152]{2,1,0:T(8,128)(2,1)S(1)}, u32[]{:S(2)}, u32[]{:S(2)}) %all-to-all-start.2) | async-done | bytes 1032224 | tf_op jit(solution)/shard_map/all_to_all | solution.py:274
  126.5 0.0 copy-start
  126.5 8.8 %shard_map.85 = bf16[448,576]{1,0:T(8,128)(2,1)S(1)} custom-call(bf16[448,1152]{1,0:T(8,128)(2,1)S(1)} %bitcast.13, f32[3,1152]{1,0:T(4,128)S(1)} %bitcast.15, bf16[1728,1152]{1,0:T(8,128)(2,1)} %bitcast.19, s32[448,1]{1,0:T(8,128)S(1)} %add_select_fusion.rows_ref, s32[1,448]{1,0:T(1,128)S(1)} %and_select_fusion.cols_ref), custom_call_target="tpu_custom_call" | custom-call | tf_op jit(solution)/shard_map/pallas_call | solution.py:203
  135.3 13.6 %all_to_all.20.mixed_ref = bf16[8,56,576]{2,1,0:T(8,128)(2,1)S(1)} all-to-all(bf16[8,56,576]{2,1,0:T(8,128)(2,1)S(1)} %bitcast.14), channel_id=1, replica_groups=mesh['dp'=32,'seq'=8] {'seq'}, dimensions={0} | all-to-all | bytes 1032192 | tf_op jit(solution)/shard_map/all_to_all | solution.py:278
  148.9 0.0 copy-done
  148.9 4.1 %shard_map.86 = bf16[7,64,1152]{2,1,0:T(8,128)(2,1)} custom-call(bf16[8,56,576]{2,1,0:T(8,128)(2,1)S(1)} %all_to_all.20.mixed_ref, bf16[8,56,1152]{2,1,0:T(8,128)(2,1)} %shard_map.84.after_ref, f32[3,1152]{1,0:T(4,128)S(1)} %bitcast.16, bf16[576,1152]{1,0:T(8,128)(2,1)S(1)} %copy-done), custom_call_target="tpu_custom_call" | custom-call | tf_op jit(solution)/shard_map/pallas_call | solution.py:233
  (8 shorter events, 0.1 us)
Async XLA Ops:
  3.8 12.2 %copy-start.2 = (s32[32,13]{0,1:T(8,128)S(1)}, s32[32,13]{0,1:T(8,128)}, u32[]{:S(2)}) copy-start(s32[32,13]{0,1:T(8,128)} %param.11) | copy-start | bytes 4996
  3.8 12.2 %copy-start.3 = (s32[32]{0:T(128)S(1)}, s32[32]{0:T(128)}, u32[]{:S(2)}) copy-start(s32[32]{0:T(128)} %param.10) | copy-start | bytes 388
  3.8 57.0 %all-to-all-start = ((bf16[32,13,2,1152]{3,2,1,0:T(2,128)(2,1)}), bf16[32,13,2,1152]{3,2,1,0:T(2,128)(2,1)S(1)}, u32[]{:S(2)}, u32[]{:S(2)}) async-start(bf16[32,13,2,1152]{3,2,1,0:T(2,128)(2,1)} %shard_map.82), calls=%async_computation | async-start | bytes 3833856 | tf_op jit(solution)/shard_map/all_to_all | solution.py:258
  60.8 8.1 %copy-start.1 = (f32[1,6,1152]{2,0,1:T(1,128)S(1)}, f32[1,6,1152]{2,0,1:T(1,128)}, u32[]{:S(2)}) copy-start(f32[1,6,1152]{2,0,1:T(1,128)} %param.9) | copy-start | bytes 82948
  62.7 31.0 %all-to-all-start.1 = ((bf16[32,7,2,1152]{3,2,1,0:T(2,128)(2,1)}), bf16[32,7,2,1152]{3,2,1,0:T(2,128)(2,1)S(1)}, u32[]{:S(2)}, u32[]{:S(2)}) async-start(bf16[32,7,2,1152]{3,2,1,0:T(2,128)(2,1)} %bitcast.1), calls=%async_computation.1 | async-start | bytes 2064384 | tf_op jit(solution)/shard_map/all_to_all | solution.py:260
  103.5 22.9 %all-to-all-start.2 = ((bf16[8,56,1152]{2,1,0:T(8,128)(2,1)}), bf16[8,56,1152]{2,1,0:T(8,128)(2,1)S(1)}, u32[]{:S(2)}, u32[]{:S(2)}) async-start(bf16[8,56,1152]{2,1,0:T(8,128)(2,1)} %shard_map.84.after_ref), calls=%async_computation.2 | async-start | bytes 2064384 | tf_op jit(solution)/shard_map/all_to_all | solution.py:274
  126.5 22.4 %copy-start = (bf16[576,1152]{1,0:T(8,128)(2,1)S(1)}, bf16[576,1152]{1,0:T(8,128)(2,1)}, u32[]{:S(2)}) copy-start(bf16[576,1152]{1,0:T(8,128)(2,1)} %wo_ref.1) | copy-start | bytes 3981316

commit v4 on v3

v4 whole, which is shorter than its diff:
```python
import functools
import math

import jax
import jax.numpy as jnp
from jax import lax
from jax.experimental import pallas as pl
from jax.experimental.pallas import tpu as pltpu
from jax.sharding import PartitionSpec as P

HEADS = 8
HEAD_DIM = 72
HD = HEADS * HEAD_DIM
SECTION = 640
NFD = 7
EPS = 1e-06
LOW = -1e30
NT = (((1,), (1,)), ((), ()))
VMEM = pl.BlockSpec(memory_space=pltpu.VMEM)
SMEM = pl.BlockSpec(memory_space=pltpu.SMEM)


def limit(mib):
    return pltpu.CompilerParams(vmem_limit_bytes=mib * 1024 * 1024)


def spread_kernel(x_ref, o_ref):
    slots = x_ref.shape[0]
    for q in range(slots):
        o_ref[:, q] = x_ref[q].reshape(o_ref.shape[0], 2, x_ref.shape[2])


def spread_pieces(slot_tokens, groups):
    slots, patches, width = slot_tokens.shape
    steps = 4
    return pl.pallas_call(
        spread_kernel,
        out_shape=jax.ShapeDtypeStruct((groups, slots, 2, width), slot_tokens.dtype),
        grid=(steps,),
        in_specs=[pl.BlockSpec((slots, patches // steps, width), lambda i: (0, i, 0))],
        out_specs=pl.BlockSpec((groups // steps, slots, 2, width), lambda i: (i, 0, 0, 0)),
        compiler_params=limit(63),
    )(slot_tokens)


def choose_kernel(index_ref, x_ref, o_ref):
    unroll = 8

    def body(i, carry):
        for j in range(unroll):
            o_ref[i * unroll + j] = x_ref[index_ref[i * unroll + j]]
        return carry

    lax.fori_loop(0, o_ref.shape[0] // unroll, body, 0)


def choose_pieces(spread, index):
    return pl.pallas_call(
        choose_kernel,
        out_shape=jax.ShapeDtypeStruct((index.shape[0],) + spread.shape[1:], spread.dtype),
        in_specs=[SMEM, VMEM],
        out_specs=VMEM,
        compiler_params=limit(26),
    )(index, spread)


def normalize(load, mod_ref, base, normed_ref):
    step = 16
    scale = 1.0 + mod_ref[base + 1 : base + 2, :]
    shift = mod_ref[base : base + 1, :]
    for at in range(0, normed_ref.shape[0], step):
        values = load(at, step).astype(jnp.float32)
        center = values - jnp.mean(values, axis=-1, keepdims=True)
        spread = jnp.mean(center * center, axis=-1, keepdims=True)
        normed_ref[at : at + step] = (center * lax.rsqrt(spread + EPS) * scale + shift).astype(jnp.bfloat16)


def project_qkv(normed_ref, w_ref, qkv_ref):
    normed = normed_ref[...]
    for part in range(3):
        start = part * SECTION
        qkv_ref[:, start + SECTION - 128 : start + SECTION] = jnp.zeros((normed.shape[0], 128), jnp.bfloat16)
    rows = normed.shape[0] // 2
    for at in range(0, 2 * rows, rows):
        full = lax.dot_general(normed[at : at + rows], w_ref[...], NT, preferred_element_type=jnp.float32)
        for part in range(3):
            qkv_ref[at : at + rows, part * SECTION : part * SECTION + HD] = full[
                :, part * HD : (part + 1) * HD
            ].astype(jnp.bfloat16)


def attend(groups, group_of, qkv_ref, s_ref, p_ref, mix_ref):
    factor = math.log2(math.e) / math.sqrt(HEAD_DIM)
    lane = lax.broadcasted_iota(jnp.int32, (1, 256), 1)
    tasks = [(h, start, size) for start, size in groups for h in range(HEADS)]

    def window(h):
        base = (HEAD_DIM * h) // 128 * 128
        low = HEAD_DIM * h - base
        return base, (lane >= low) & (lane < low + HEAD_DIM)

    def scores(t):
        h, start, size = tasks[t]
        base, own = window(h)
        rows = pl.ds(start, size)
        q = jnp.where(own, qkv_ref[rows, pl.ds(base, 256)], jnp.bfloat16(0))
        k = qkv_ref[rows, pl.ds(SECTION + base, 256)]
        s_ref[t % 2, :size, :size] = lax.dot_general(q, k, NT, preferred_element_type=jnp.float32)

    def weights(t):
        h, start, size = tasks[t]
        same = group_of(lax.broadcasted_iota(jnp.int32, (size, 1), 0)) == group_of(
            lax.broadcasted_iota(jnp.int32, (1, size), 1)
        )
        s = jnp.where(same, s_ref[t % 2, :size, :size], LOW)
        raised = jnp.exp2((s - jnp.max(s, axis=-1, keepdims=True)) * factor)
        inverse = 1.0 / jnp.sum(raised, axis=-1, keepdims=True)
        p_ref[t % 2, :size, :size] = (raised * inverse).astype(jnp.bfloat16)

    def mixing(t):
        h, start, size = tasks[t]
        base, own = window(h)
        rows = pl.ds(start, size)
        mixed = jnp.dot(
            p_ref[t % 2, :size, :size],
            qkv_ref[rows, pl.ds(2 * SECTION + base, 256)],
            preferred_element_type=jnp.float32,
        ).astype(jnp.bfloat16)
        mix_ref[rows, pl.ds(base, 256)] = jnp.where(own, mixed, mix_ref[rows, pl.ds(base, 256)])

    scores(0)
    for t in range(len(tasks)):
        if t + 1 < len(tasks):
            scores(t + 1)
        weights(t)
        mixing(t)


def spatial_kernel(
    groups, group_of, x_ref, mod_ref, w_ref, wo_ref, o_ref, frames_ref, normed_ref, qkv_ref, s_ref, p_ref, mix_ref
):
    frame_count = x_ref.shape[1]
    patches = frames_ref.shape[0] // frame_count

    def load(at, step):
        k, w = at // patches, at % patches // 2
        rows = x_ref[w : w + step // 2, k].reshape(step, x_ref.shape[3])
        frames_ref[at : at + step] = rows
        return rows

    normalize(load, mod_ref, 0, normed_ref)
    project_qkv(normed_ref, w_ref, qkv_ref)
    mix_ref[...] = jnp.zeros_like(mix_ref)
    attend(groups, group_of, qkv_ref, s_ref, p_ref, mix_ref)
    shards = o_ref.shape[0]
    widest = patches // shards
    for start, size in groups:
        rows = pl.ds(start, size)
        projected = jnp.dot(mix_ref[rows, 0:HD], wo_ref[...], preferred_element_type=jnp.float32)
        after = (frames_ref[rows, :].astype(jnp.float32) + mod_ref[2:3, :] * projected).astype(jnp.bfloat16)
        for at in range(0, size, widest):
            k, j = (start + at) // patches, (start + at) % patches // widest
            o_ref[j, k * widest : (k + 1) * widest, :] = after[at : at + widest]


def spatial_block(gathered, mod, w_qkv, w_out, groups, group_of, shards):
    pieces, frame_count, piece, width = gathered.shape
    rows = pieces * frame_count * piece
    biggest = max(size for _, size in groups)
    return pl.pallas_call(
        functools.partial(spatial_kernel, groups, group_of),
        out_shape=jax.ShapeDtypeStruct((shards, rows // shards, width), gathered.dtype),
        in_specs=[VMEM] * 4,
        out_specs=VMEM,
        scratch_shapes=[
            pltpu.VMEM((rows, width), jnp.bfloat16),
            pltpu.VMEM((rows, width), jnp.bfloat16),
            pltpu.VMEM((rows, 3 * SECTION), jnp.bfloat16),
            pltpu.VMEM((2, biggest, biggest), jnp.float32),
            pltpu.VMEM((2, biggest, biggest), jnp.bfloat16),
            pltpu.VMEM((rows, SECTION), jnp.bfloat16),
        ],
        compiler_params=limit(28),
    )(gathered, mod, w_qkv, w_out)


def temporal_kernel(
    groups, group_of, x_ref, mod_ref, w_ref, o_ref, normed_ref, qkv_ref, s_ref, p_ref, mix_ref
):
    normalize(lambda at, step: x_ref[at : at + step], mod_ref, 3, normed_ref)
    project_qkv(normed_ref, w_ref, qkv_ref)
    mix_ref[...] = jnp.zeros_like(mix_ref)
    attend(groups, group_of, qkv_ref, s_ref, p_ref, mix_ref)
    o_ref[...] = mix_ref[:, 0:HD]


def temporal_block(x, mod, w_qkv, groups, group_of):
    rows, width = x.shape
    biggest = max(size for _, size in groups)
    return pl.pallas_call(
        functools.partial(temporal_kernel, groups, group_of),
        out_shape=jax.ShapeDtypeStruct((rows, HD), x.dtype),
        in_specs=[VMEM] * 3,
        out_specs=VMEM,
        scratch_shapes=[
            pltpu.VMEM((rows, width), jnp.bfloat16),
            pltpu.VMEM((rows, 3 * SECTION), jnp.bfloat16),
            pltpu.VMEM((2, biggest, biggest), jnp.float32),
            pltpu.VMEM((2, biggest, biggest), jnp.bfloat16),
            pltpu.VMEM((rows, SECTION), jnp.bfloat16),
        ],
        compiler_params=limit(28),
    )(x, mod, w_qkv)


def final_kernel(mixed_ref, after_ref, mod_ref, wo_ref, o_ref):
    frame_count, patches, _ = o_ref.shape
    shards = after_ref.shape[0]
    widest = patches // shards
    rows = after_ref.shape[1]
    half = shards // 2
    for first in range(0, shards, half):
        mixed = mixed_ref[first : first + half].reshape(half * rows, mixed_ref.shape[2])
        projected = jnp.dot(mixed, wo_ref[...], preferred_element_type=jnp.float32)
        for j in range(first, first + half):
            part = projected[(j - first) * rows : (j - first + 1) * rows]
            result = (after_ref[j].astype(jnp.float32) + mod_ref[5:6, :] * part).astype(jnp.bfloat16)
            for k in range(frame_count):
                o_ref[k, j * widest : (j + 1) * widest, :] = result[k * widest : (k + 1) * widest]


def final_block(mixed, after, mod, w_out):
    shards, rows, width = after.shape
    return pl.pallas_call(
        final_kernel,
        out_shape=jax.ShapeDtypeStruct((NFD, shards * rows // NFD, width), after.dtype),
        in_specs=[VMEM] * 4,
        out_specs=VMEM,
        compiler_params=limit(26),
    )(mixed, after, mod, w_out)


def source_index(counts, dest):
    groups, slots = dest.shape
    slot_ids = jnp.arange(slots, dtype=jnp.int32)
    live = slot_ids[None, :] < counts[:, None]
    targets = jnp.where(live, dest, -1).reshape(-1)
    wanted = jnp.arange(groups * NFD, dtype=jnp.int32)
    anchors = jnp.arange(groups * slots, dtype=jnp.int32)
    return jnp.sum(jnp.where(targets[None, :] == wanted[:, None], anchors[None, :], 0), axis=1)


def on_device(slot_tokens, modulation, counts, dest, qkv_spatial, out_spatial, qkv_temporal, out_temporal):
    groups = lax.axis_size("dp")
    shards = lax.axis_size("seq")
    slots, patches, width = slot_tokens.shape
    piece = patches // groups
    spread = lax.all_to_all(spread_pieces(slot_tokens, groups), "dp", split_axis=0, concat_axis=0, tiled=True)
    spread, mod, index = lax.optimization_barrier((spread, modulation[0], source_index(counts, dest)))
    chosen = choose_pieces(spread.reshape(groups * slots, piece, width), index)
    gathered = lax.all_to_all(
        chosen.reshape(groups, NFD, piece, width), "dp", split_axis=0, concat_axis=0, tiled=True
    )
    shift = patches.bit_length() - 1
    after = spatial_block(
        gathered,
        mod,
        qkv_spatial.T,
        out_spatial,
        ((0, 4 * patches), (4 * patches, 3 * patches)),
        lambda row: row >> shift,
        shards,
    )
    widest = patches // shards
    moved = lax.all_to_all(after, "seq", split_axis=0, concat_axis=0, tiled=True)
    mixed = temporal_block(
        moved.reshape(NFD * patches, width),
        mod,
        qkv_temporal.T,
        ((0, NFD * patches),),
        lambda row: row & (widest - 1),
    )
    back = lax.all_to_all(
        mixed.reshape(shards, NFD * widest, HD), "seq", split_axis=0, concat_axis=0, tiled=True
    )
    return final_block(back, after, mod, out_temporal)


def solution(mesh):
    in_specs = (P("dp", "seq", None), P("dp", None, None), P(), P(), P(), P(), P(), P())
    return jax.shard_map(
        on_device, mesh=mesh, in_specs=in_specs, out_specs=P("dp", "seq", None), check_vma=False
    )
```

time: 153 us -> 145 us (0.948)
  blocking collectives: 13.6 us -> 67.3 us
  waiting for transfers between devices: 83.9 us -> 44.4 us
  starting transfers between devices: 26.5 us -> 12.2 us
  Pallas kernels: 28.5 us -> 20 us
    all_to_all x0 -> x2, blocking collectives: none -> 53.6 us  [the longest x1 30.9 us: on_device(): lax.all_to_all(chosen.reshape(groups, NFD, piece, width), 'dp', split_axi...]
    all_to_all x2 -> x0, waiting for transfers between devices: 39.5 us -> none  [the longest x1 24.7 us: on_device(): lax.all_to_all(chosen.reshape(groups, NFD, piece, width), 'dp', split_axi...]
    all_to_all x2 -> x0, starting transfers between devices: 14.3 us -> none  [the longest x1 8.14 us: on_device(): lax.all_to_all(after, 'seq', split_axis=0, concat_axis=0, tiled=True)]
    pallas_call x2, Pallas kernels: 18.6 us -> 13.2 us  [the longest x1 6.81 us: spatial_block(): pl.pallas_call(functools.partial(spatial_kernel, groups, group_of), out_s...]
    pallas_call x1, Pallas kernels: 4.13 us -> 2 us  [final_block(): pl.pallas_call(final_kernel, out_shape=jax.ShapeDtypeStruct((NFD, shards...]
  transfers between devices with their start and end apart: 3 -> 1, of which waited for: 3 -> 1; matrix products, arithmetic and copies ran while one was open for 0% -> 0% of each run, Pallas kernels for 0% -> 0%
where the time goes in v4:
time: 145 us; the launch traced here: 144 us
  blocking collectives  67.3 us (46%)
  waiting for transfers between devices  44.4 us (31%)
  Pallas kernels  20 us (14%)
  starting transfers between devices  12.2 us (8%)
    all_to_all x1, waiting for transfers between devices, on_device(): lax.all_to_all(spread_pieces(slot_tokens, groups), 'dp', split_axis=0, co...  44.4 us
    all_to_all x1, blocking collectives, on_device(): lax.all_to_all(chosen.reshape(groups, NFD, piece, width), 'dp', split_axi...  30.9 us
    all_to_all x1, blocking collectives, on_device(): lax.all_to_all(after, 'seq', split_axis=0, concat_axis=0, tiled=True)  22.7 us
    all_to_all x1, blocking collectives, on_device(): lax.all_to_all(mixed.reshape(shards, NFD * widest, HD), 'seq', split_axis...  13.6 us
    all_to_all x1, starting transfers between devices, on_device(): lax.all_to_all(spread_pieces(slot_tokens, groups), 'dp', split_axis=0, co...  12.2 us
    pallas_call x1, Pallas kernels, spatial_block(): pl.pallas_call(functools.partial(spatial_kernel, groups, group_of), out_s...  6.81 us
    pallas_call x1, Pallas kernels, temporal_block(): pl.pallas_call(functools.partial(temporal_kernel, groups, group_of), out_...  6.41 us
    pallas_call x1, Pallas kernels, spread_pieces(): pl.pallas_call(spread_kernel, out_shape=jax.ShapeDtypeStruct((groups, slo...  3.81 us
  transfers between devices with their start and end apart: 1, of which 1 were waited for; matrix products, arithmetic and copies ran while one was open for 0% of the time, Pallas kernels for 0%

profile of v4, /device:TPU:1, one launch (start us, length us, event | category | flops | bytes accessed | tf_op | source)
XLA Modules:
  0.0 144.3 jit_solution(10715927256643107533)
XLA Ops:
  0.0 3.8 %shard_map.82 = bf16[32,13,2,1152]{3,2,1,0:T(2,128)(2,1)} custom-call(bf16[13,64,1152]{2,1,0:T(8,128)(2,1)} %x_ref.1), custom_call_target="tpu_custom_call" | custom-call | tf_op jit(solution)/shard_map/pallas_call | solution.py:36
  3.8 0.0 copy-start.4
  3.8 0.0 copy-start.5
  3.8 0.0 copy-start.6
  3.8 0.0 copy-start.2
  3.8 12.2 %all-to-all-start = ((bf16[32,13,2,1152]{3,2,1,0:T(2,128)(2,1)}), bf16[32,13,2,1152]{3,2,1,0:T(2,128)(2,1)S(1)}, u32[]{:S(2)}, u32[]{:S(2)}) async-start(bf16[32,13,2,1152]{3,2,1,0:T(2,128)(2,1)} %shard_map.82), calls=%async_computation | async-start | bytes 3833856 | tf_op jit(solution)/shard_map/all_to_all | solution.py:258
  16.0 0.0 copy-done.4
  16.0 0.0 copy-done.5
  16.0 0.0 copy-done.6
  16.1 0.1 copy.10
  16.1 0.1 eq.15
  16.2 0.1 select_reduce_fusion.index_ref
  16.4 44.4 %all-to-all-done = bf16[32,13,2,1152]{3,2,1,0:T(2,128)(2,1)S(1)} async-done(((bf16[32,13,2,1152]{3,2,1,0:T(2,128)(2,1)}), bf16[32,13,2,1152]{3,2,1,0:T(2,128)(2,1)S(1)}, u32[]{:S(2)}, u32[]{:S(2)}) %all-to-all-start) | async-done | bytes 1916960 | tf_op jit(solution)/shard_map/all_to_all | solution.py:258
  60.8 0.0 copy-start
  60.8 0.9 shard_map.83
  61.8 30.9 %all_to_all.20.x_ref = bf16[32,7,2,1152]{3,2,1,0:T(2,128)(2,1)S(1)} all-to-all(bf16[32,7,2,1152]{3,2,1,0:T(2,128)(2,1)S(1)} %bitcast.11), channel_id=1, replica_groups=mesh['dp'=32,'seq'=8] {'dp'}, dimensions={0} | all-to-all | bytes 2064384 | tf_op jit(solution)/shard_map/all_to_all | solution.py:261
  92.7 0.0 copy-done.2
  92.7 0.0 copy-done
  92.7 0.0 copy-start.1
  92.7 6.8 %shard_map.84.after_ref = bf16[8,56,1152]{2,1,0:T(8,128)(2,1)S(1)} custom-call(bf16[32,7,2,1152]{3,2,1,0:T(2,128)(2,1)S(1)} %all_to_all.20.x_ref, f32[6,1152]{1,0:T(8,128)S(1)} %bitcast.15, bf16[1728,1152]{1,0:T(8,128)(2,1)S(1)} %bitcast.12, bf16[576,1152]{1,0:T(8,128)(2,1)S(1)} %copy-done.2), custom_call_target="tpu_custom_call" | custom-call | tf_op jit(solution)/shard_map/pallas_call | solution.py:170
  99.5 22.7 %all_to_all.21 = bf16[8,56,1152]{2,1,0:T(8,128)(2,1)S(1)} all-to-all(bf16[8,56,1152]{2,1,0:T(8,128)(2,1)S(1)} %shard_map.84.after_ref), channel_id=1, replica_groups=mesh['dp'=32,'seq'=8] {'seq'}, dimensions={0} | all-to-all | bytes 2064384 | tf_op jit(solution)/shard_map/all_to_all | solution.py:275
  122.2 0.0 copy-done.1
  122.2 0.0 copy-start.3
  122.2 6.4 %shard_map.85 = bf16[448,576]{1,0:T(8,128)(2,1)S(1)} custom-call(bf16[448,1152]{1,0:T(8,128)(2,1)S(1)} %bitcast.10, f32[6,1152]{1,0:T(8,128)S(1)} %bitcast.16, bf16[1728,1152]{1,0:T(8,128)(2,1)S(1)} %bitcast.13), custom_call_target="tpu_custom_call" | custom-call | tf_op jit(solution)/shard_map/pallas_call | solution.py:200
  128.7 13.6 %all_to_all.22.mixed_ref = bf16[8,56,576]{2,1,0:T(8,128)(2,1)S(1)} all-to-all(bf16[8,56,576]{2,1,0:T(8,128)(2,1)S(1)} %bitcast.14), channel_id=1, replica_groups=mesh['dp'=32,'seq'=8] {'seq'}, dimensions={0} | all-to-all | bytes 1032192 | tf_op jit(solution)/shard_map/all_to_all | solution.py:283
  142.3 0.0 copy-done.3
  142.3 2.0 %shard_map.86 = bf16[7,64,1152]{2,1,0:T(8,128)(2,1)} custom-call(bf16[8,56,576]{2,1,0:T(8,128)(2,1)S(1)} %all_to_all.22.mixed_ref, bf16[8,56,1152]{2,1,0:T(8,128)(2,1)S(1)} %shard_map.84.after_ref, f32[6,1152]{1,0:T(8,128)S(1)} %bitcast.17, bf16[576,1152]{1,0:T(8,128)(2,1)S(1)} %copy-done.3), custom_call_target="tpu_custom_call" | custom-call | tf_op jit(solution)/shard_map/pallas_call | solution.py:234
  (2 shorter events, 0.0 us)
Async XLA Ops:
  3.8 12.2 %copy-start.4 = (f32[1,6,1152]{2,0,1:T(1,128)S(1)}, f32[1,6,1152]{2,0,1:T(1,128)}, u32[]{:S(2)}) copy-start(f32[1,6,1152]{2,0,1:T(1,128)} %param.9) | copy-start | bytes 82948
  3.8 12.2 %copy-start.5 = (s32[32,13]{0,1:T(8,128)S(1)}, s32[32,13]{0,1:T(8,128)}, u32[]{:S(2)}) copy-start(s32[32,13]{0,1:T(8,128)} %param.11) | copy-start | bytes 4996
  3.8 12.2 %copy-start.6 = (s32[32]{0:T(128)S(1)}, s32[32]{0:T(128)}, u32[]{:S(2)}) copy-start(s32[32]{0:T(128)} %param.10) | copy-start | bytes 388
  3.8 88.9 %copy-start.2 = (bf16[576,1152]{1,0:T(8,128)(2,1)S(1)}, bf16[576,1152]{1,0:T(8,128)(2,1)}, u32[]{:S(2)}) copy-start(bf16[576,1152]{1,0:T(8,128)(2,1)} %wo_ref.2) | copy-start | bytes 3981316
  3.8 57.0 %all-to-all-start = ((bf16[32,13,2,1152]{3,2,1,0:T(2,128)(2,1)}), bf16[32,13,2,1152]{3,2,1,0:T(2,128)(2,1)S(1)}, u32[]{:S(2)}, u32[]{:S(2)}) async-start(bf16[32,13,2,1152]{3,2,1,0:T(2,128)(2,1)} %shard_map.82), calls=%async_computation | async-start | bytes 3833856 | tf_op jit(solution)/shard_map/all_to_all | solution.py:258
  60.8 31.9 %copy-start = (bf16[1152,1728]{0,1:T(8,128)(2,1)S(1)}, bf16[1152,1728]{0,1:T(8,128)(2,1)}, u32[]{:S(2)}) copy-start(bf16[1152,1728]{0,1:T(8,128)(2,1)} %param.12) | copy-start | bytes 11943940
  92.7 29.5 %copy-start.1 = (bf16[1152,1728]{0,1:T(8,128)(2,1)S(1)}, bf16[1152,1728]{0,1:T(8,128)(2,1)}, u32[]{:S(2)}) copy-start(bf16[1152,1728]{0,1:T(8,128)(2,1)} %param.14) | copy-start | bytes 11943940
  122.2 20.0 %copy-start.3 = (bf16[576,1152]{1,0:T(8,128)(2,1)S(1)}, bf16[576,1152]{1,0:T(8,128)(2,1)}, u32[]{:S(2)}) copy-start(bf16[576,1152]{1,0:T(8,128)(2,1)} %wo_ref.3) | copy-start | bytes 3981316
